TPU v7x, 512 devices: a whole 4x4x16 slice. The times are simulated.
512 devices in a mesh: row: 32 (over x, y, core), col: 16 (over z).
Axes of the slice: x: 4, y: 4, z: 16, core: 2. Of those that a mesh axis runs over, the one named last changes fastest.
Arguments:
- features: bfloat16 [65536, 256], P('col', 'row'), may hold values from -6 to 6
- weight: bfloat16 [256, 256], replicated, may hold values from -0.375 to 0.375
- adj_values: bfloat16 [32, 16, 96, 128, 128], P('row', 'col'), may hold values from -0.0625 to 0.0625
- block_rows: int32 [32, 16, 96], P('row', 'col'), may hold values from 0 to 15, as said below
- block_cols: int32 [32, 16, 96], P('row', 'col'), may hold values from 0 to 31
- block_counts: int32 [32, 16], P('row', 'col'), may hold values from 1 to 96, as said below
- cotangent: bfloat16 [65536, 256], P(('row', 'col')), may hold values from -6 to 6
Outputs:
- output: bfloat16 [65536, 256], P(('row', 'col'))
- grad_weight: float32 [256, 256], replicated
- grad_features: bfloat16 [65536, 256], P('col', 'row')
Inputs may be any that keep to these rules, and one draw needn't show every extreme that they name: Within one tile the pairs (block_rows, block_cols) over all 96 slots are distinct. `block_counts`: some tile holds exactly 96 live blocks and some other tile exactly one in every draw.
All inputs are finite; a program needn't handle non-finite values.
Results may differ from a plain program's by a relative error of at most 0.029.
Values may be sent and summed in bfloat16 or wider, within the bound.
A program may use at most 64 MiB of HBM per device.

v0:
```python
import math

import jax
import jax.numpy as jnp
from jax import lax
from jax.sharding import PartitionSpec as P

RB = 16


def block_product(tile_values, tile_rows, tile_cols, live_count, panels, out_blocks, transposed):
    padded = tile_values.shape[0]
    blocks_turn = math.gcd(padded, 16)
    block_size = panels.shape[1]
    columns = panels.shape[2]
    turns_needed = (live_count + blocks_turn - 1) // blocks_turn

    def step(turn_index, running):
        offset = turn_index * blocks_turn
        values_now = lax.dynamic_slice_in_dim(tile_values, offset, blocks_turn, 0)
        row_ids = lax.dynamic_slice_in_dim(tile_rows, offset, blocks_turn, 0)
        col_ids = lax.dynamic_slice_in_dim(tile_cols, offset, blocks_turn, 0)
        is_live = offset + jnp.arange(blocks_turn, dtype=jnp.int32) < live_count
        if transposed:
            picked = jnp.take(panels, row_ids, axis=0)
            product = jnp.einsum(
                "bij,bif->bjf", values_now, picked, preferred_element_type=jnp.float32
            )
            target_ids = col_ids
        else:
            picked = jnp.take(panels, col_ids, axis=0)
            product = jnp.einsum(
                "bij,bjf->bif", values_now, picked, preferred_element_type=jnp.float32
            )
            target_ids = row_ids
        contribution = jnp.where(is_live[:, None, None], product, 0.0)
        return running.at[target_ids].add(contribution)

    start_sum = jnp.zeros((out_blocks, block_size, columns), jnp.float32)
    return lax.fori_loop(0, turns_needed, step, start_sum)


def shards(features, weight, adj_values, block_rows, block_cols, block_counts, cotangent):
    tile_values = adj_values[0, 0]
    tile_rows = block_rows[0, 0]
    tile_cols = block_cols[0, 0]
    live_count = block_counts[0, 0]
    block_size = tile_values.shape[1]
    col_blocks = features.shape[0] // block_size
    node_total = col_blocks * block_size * lax.axis_size("col")
    panel_part = lax.all_gather(features, "row", axis=1, tiled=True)
    panels = panel_part.reshape(col_blocks, block_size, panel_part.shape[1])
    partial_value = block_product(tile_values, tile_rows, tile_cols, live_count, panels, RB, False)
    partial_value = partial_value.reshape(RB * block_size, partial_value.shape[2])
    aggregated = lax.psum_scatter(
        partial_value.astype(jnp.bfloat16), "col", scatter_dimension=0, tiled=True
    )
    preact = jnp.dot(aggregated, weight, preferred_element_type=jnp.float32)
    output = jax.nn.silu(preact).astype(jnp.bfloat16)
    sigmoid_pre = jax.nn.sigmoid(preact)
    slopes = sigmoid_pre * (1.0 + preact * (1.0 - sigmoid_pre))
    deltas = (cotangent.astype(jnp.float32) * slopes).astype(jnp.bfloat16)
    local_grad = jnp.dot(aggregated.T, deltas, preferred_element_type=jnp.float32)
    grad_weight = lax.psum(local_grad, ("row", "col")) * (1.0 / math.sqrt(node_total))
    backward = jnp.dot(deltas, weight.T, preferred_element_type=jnp.float32).astype(jnp.bfloat16)
    back_slab = lax.all_gather(backward, "col", axis=0, tiled=True)
    back_panels = back_slab.reshape(RB, block_size, back_slab.shape[1])
    column_terms = block_product(
        tile_values, tile_rows, tile_cols, live_count, back_panels, col_blocks, True
    )
    column_terms = column_terms.reshape(col_blocks * block_size, column_terms.shape[2])
    grad_features = lax.psum_scatter(
        column_terms.astype(jnp.bfloat16), "row", scatter_dimension=1, tiled=True
    )
    return (output, grad_weight, grad_features)


def solution(mesh):
    return jax.shard_map(
        shards,
        mesh=mesh,
        in_specs=(
            P("col", "row"),
            P(),
            P("row", "col", None, None, None),
            P("row", "col", None),
            P("row", "col", None),
            P("row", "col"),
            P(("row", "col"), None),
        ),
        out_specs=(P(("row", "col"), None), P(), P("col", "row")),
        check_vma=False,
    )
```

profile of v0, /device:TPU:1, one launch (start us, length us, event | category | flops | bytes accessed | tf_op | source)
XLA Modules:
  0.0 846.8 jit_solution(3140927563884392423)
XLA Ops:
  7.2 0.0 all-gather.3.cloned.1.call-start
  7.2 0.7 all-gather.3.cloned.1.call-update
  7.9 0.0 reduce-scatter.3.cloned.1.call-start
  8.6 67.4 %all-gather.3.cloned.1.call-done = bf16[4096,256]{0,1:T(8,128)(2,1)} async-done(((bf16[4096,8]{0,1:T(8,128)(2,1)}), bf16[4096,256]{0,1:T(8,128)(2,1)}) %all-gather.3.cloned.1.call-update) | async-done | bytes 2097168 | tf_op jit(solution)/shard_map/all_gather | solution.py:51
  76.1 4.1 copy.11
  80.1 1.5 broadcast_in_dim.58
  81.7 36.0 %while.20 = (s32[]{:T(128)}, f32[16,128,256]{2,1,0:T(8,128)}, s32[]{:T(128)}, s32[96]{0:T(128)S(1)}, s32[]{:T(128)}, /*index=5*/bf16[96,128,128]{2,1,0:T(8,128)(...) while((s32[]{:T(128)}, f32[16,128,256]{2,1,0:T(8,128)}, ...), condition=%wide.region_2.3_spmd, body=%wide.region_0.2_spmd.sunk | while | flops 135791792 | bytes 12063415 | solution.py:40
  81.7 0.7 compare_and_fusion.4
  82.4 2.2 gather_fusion
  84.6 1.5 convolution_select_fusion.4
  86.2 0.1 compare_select_fusion.8
  86.3 4.5 scatter_fusion
  90.7 0.7 compare_and_fusion.4
  91.5 2.2 gather_fusion
  93.7 1.5 convolution_select_fusion.4
  95.2 0.1 compare_select_fusion.8
  95.3 4.3 scatter_fusion
  99.7 0.7 compare_and_fusion.4
  100.4 2.2 gather_fusion
  102.6 1.5 convolution_select_fusion.4
  104.2 0.1 compare_select_fusion.8
  104.2 4.4 scatter_fusion
  108.6 0.7 compare_and_fusion.4
  109.4 2.2 gather_fusion
  111.6 1.5 convolution_select_fusion.4
  113.1 0.1 compare_select_fusion.8
  113.2 4.4 scatter_fusion
  117.6 2.8 convert_element_type.24
  120.5 0.0 all-gather.5.cloned.1.call-start
  120.6 76.3 %reduce-scatter.3.cloned.1.call-done = bf16[128,256]{1,0:T(8,128)(2,1)} async-done(((bf16[2048,256]{1,0:T(8,128)(2,1)}), bf16[128,256]{1,0:T(8,128)(2,1)}) %reduce-scatter.3.cloned.1.call-update) | async-done | bytes 65552 | tf_op jit(solution)/shard_map/reduce_scatter | solution.py:55
  196.9 1.7 multiply_convert_fusion
  198.6 0.8 convolution_convert_fusion
  199.5 0.0 all-reduce.2.cloned.1.call-start
  199.5 2.8 copy.10
  202.3 0.9 fusion.12
  203.3 0.0 reduce-scatter.5.cloned.1.call-start
  203.3 65.6 %all-gather.5.cloned.1.call-done = bf16[2048,256]{1,0:T(8,128)(2,1)} async-done(((bf16[128,256]{1,0:T(8,128)(2,1)}), bf16[2048,256]{1,0:T(8,128)(2,1)}) %all-gather.5.cloned.1.call-update) | async-done | bytes 1048592 | tf_op jit(solution)/shard_map/all_gather | solution.py:66
  269.0 2.4 broadcast_in_dim.59
  271.4 34.8 %while.21 = (s32[]{:T(128)}, f32[32,128,256]{2,1,0:T(8,128)}, s32[]{:T(128)}, s32[96]{0:T(128)S(1)}, s32[]{:T(128)}, /*index=5*/bf16[96,128,128]{1,2,0:T(8,128)(...) while((s32[]{:T(128)}, f32[32,128,256]{2,1,0:T(8,128)}, ...), condition=%wide.region_7.8_spmd, body=%wide.region_5.7_spmd.sunk | while | flops 135791792 | bytes 12063415 | solution.py:40
  271.4 0.7 compare_and_fusion.5
  272.1 1.8 gather_fusion.1
  274.0 1.5 convolution_select_fusion.5
  275.5 0.1 compare_select_fusion.9
  275.6 4.4 scatter_fusion.1
  280.1 0.7 compare_and_fusion.5
  280.8 1.8 gather_fusion.1
  282.7 1.6 convolution_select_fusion.5
  284.2 0.1 compare_select_fusion.9
  284.3 4.4 scatter_fusion.1
  288.7 0.7 compare_and_fusion.5
  289.5 1.8 gather_fusion.1
  291.3 1.5 convolution_select_fusion.5
  292.9 0.1 compare_select_fusion.9
  293.0 4.6 scatter_fusion.1
  297.5 0.7 compare_and_fusion.5
  298.3 1.8 gather_fusion.1
  300.1 1.5 convolution_select_fusion.5
  301.7 0.1 compare_select_fusion.9
  301.7 4.4 scatter_fusion.1
  306.2 2.5 convert_element_type.30
  308.6 2.9 copy.15
  311.6 426.5 %all-reduce.2.cloned.1.call-done = f32[256,256]{1,0:T(8,128)} async-done(((f32[256,256]{1,0:T(8,128)}), f32[256,256]{1,0:T(8,128)}) %all-reduce.2.cloned.1.call-update) | async-done | bytes 262160 | tf_op jit(solution)/shard_map/psum | solution.py:64
  738.1 1.7 broadcast_multiply_fusion
  739.8 100.5 %reduce-scatter.5.cloned.1.call-done = bf16[4096,8]{0,1:T(8,128)(2,1)} async-done(((bf16[4096,256]{0,1:T(8,128)(2,1)}), bf16[4096,8]{0,1:T(8,128)(2,1)}) %reduce-scatter.5.cloned.1.call-update) | async-done | bytes 65552 | tf_op jit(solution)/shard_map/reduce_scatter | solution.py:72
  (24 shorter events, 0.1 us)
Async XLA Ops:
  7.2 189.7 %copy-start = (bf16[256,256]{1,0:T(8,128)(2,1)S(1)}, bf16[256,256]{1,0:T(8,128)(2,1)}, u32[]{:S(2)}) copy-start(bf16[256,256]{1,0:T(8,128)(2,1)} %param.12) | copy-start | bytes 393220
  7.2 68.9 %all-gather.3.cloned.1.call-start = ((), (), s32[]{:S(2)}) async-start(), calls=%async_computation.2 | async-start | bytes 2162688 | tf_op jit(solution)/shard_map/all_gather | solution.py:51
  7.9 189.0 %reduce-scatter.3.cloned.1.call-start = ((), (), s32[]{:S(2)}) async-start(), calls=%async_computation.3 | async-start | bytes 1114112 | tf_op jit(solution)/shard_map/reduce_scatter | solution.py:55
  80.1 1.5 copy-start.3
  80.1 1.5 copy-start.4
  117.6 79.3 %copy-start.5 = (bf16[128,256]{1,0:T(8,128)(2,1)S(1)}, bf16[128,256]{1,0:T(8,128)(2,1)}, u32[]{:S(2)}) copy-start(bf16[128,256]{1,0:T(8,128)(2,1)} %param.17) | copy-start | bytes 196612
  117.6 81.9 %copy-start.1 = (bf16[96,128,128]{2,1,0:T(8,128)(2,1)S(1)}, bf16[96,128,128]{2,1,0:T(8,128)(2,1)}, u32[]{:S(2)}) copy-start(bf16[96,128,128]{2,1,0:T(8,128)(2,1)} %get-tuple-element.328) | copy-start | bytes 9437188
  120.5 148.5 %all-gather.5.cloned.1.call-start = ((), (), s32[]{:S(2)}) async-start(), calls=%async_computation.5 | async-start | bytes 1114112 | tf_op jit(solution)/shard_map/all_gather | solution.py:66
  199.5 2.9 copy-start.2
  199.5 538.6 %all-reduce.2.cloned.1.call-start = ((), (), s32[]{:S(2)}) async-start(), calls=%async_computation.4 | async-start | bytes 524288 | tf_op jit(solution)/shard_map/psum | solution.py:64
  203.3 637.0 %reduce-scatter.5.cloned.1.call-start = ((), (), s32[]{:S(2)}) async-start(), calls=%async_computation.6 | async-start | bytes 2162688 | tf_op jit(solution)/shard_map/reduce_scatter | solution.py:72
Sparse Core Ops, SparseCore 0:
  11.1 64.8 all-gather.2
  120.6 76.2 reduce-scatter.2
  199.8 69.1 all-gather.4
  275.7 462.3 all-reduce.1
  742.9 97.3 reduce-scatter.4
where the time goes:
time: 849 us; the launch traced here: 847 us
  waiting for transfers between devices  737 us (87%)
  other arithmetic  49 us (6%)
  local copies, waits for them, and re-layouts  30 us (4%)
  matrix products  15.8 us (2%)
  between operations  14.5 us (2%)
    psum x1, waiting for transfers between devices, shards(): lax.psum(local_grad, ('row', 'col')) * (1.0 / math.sqrt(node_total))  426 us
    reduce_scatter x1, waiting for transfers between devices, shards(): lax.psum_scatter(column_terms.astype(jnp.bfloat16), 'row', scatter_dimens...  101 us
    reduce_scatter x1, waiting for transfers between devices, shards(): lax.psum_scatter(partial_value.astype(jnp.bfloat16), 'col', scatter_dimen...  76.3 us
    all_gather x1, waiting for transfers between devices, shards(): panel_part = lax.all_gather(features, 'row', axis=1, tiled=True)  67.4 us
    all_gather x1, waiting for transfers between devices, shards(): back_slab = lax.all_gather(backward, 'col', axis=0, tiled=True)  65.6 us
    scatter-add x8, other arithmetic, step(): return running.at[target_ids].add(contribution)  35.5 us
  transfers between devices with their start and end apart: 5, of which 5 were waited for; matrix products, arithmetic and copies ran while one was open for 6% of the time, Pallas kernels for 0%

commit v1 on v0

v1 whole, which is shorter than its diff:
```python
import functools
import math

import jax
import jax.numpy as jnp
from jax import lax
from jax.experimental import pallas as pl
from jax.experimental.pallas import tpu as pltpu
from jax.sharding import PartitionSpec as P

MESH = pl.DeviceIdType.MESH
VMEM_LIMIT = 56 * 2**20
NT = (((1,), (1,)), ((), ()))
TN = (((0,), (0,)), ((), ()))
DMA = pltpu.SemaphoreType.DMA
BF16, F32 = jnp.bfloat16, jnp.float32


class Place:
    def __init__(self, n_row, n_col):
        self.n_row, self.n_col = n_row, n_col
        self.chips = n_row // 2
        self.side = math.isqrt(self.chips)
        self.row, self.col = lax.axis_index("row"), lax.axis_index("col")
        self.core = lax.rem(self.row, 2)
        chip = lax.div(self.row, 2)
        self.x, self.y = lax.div(chip, self.side), lax.rem(chip, self.side)

    def chip(self, k, sign=1):
        dx, dy = lax.div(k, self.side), lax.rem(k, self.side)
        x = lax.rem(self.x + sign * dx + self.side, self.side)
        y = lax.rem(self.y + sign * dy + self.side, self.side)
        return x * self.side + y

    def at(self, row=None, col=None):
        return (self.row if row is None else row, self.col if col is None else col)

    def sibling(self):
        return self.at(row=self.row + 1 - 2 * self.core)

    def peer_row(self, k):
        return lax.rem(self.row + k, self.n_row)

    def peer_col(self, k):
        return lax.rem(self.col + k + self.n_col, self.n_col)


def signal(barrier, device):
    pl.semaphore_signal(barrier, inc=1, device_id=device, device_id_type=MESH)


def remote(src, dst, send, recv, device):
    return pltpu.make_async_remote_copy(
        src_ref=src, dst_ref=dst, send_sem=send, recv_sem=recv, device_id=device, device_id_type=MESH
    )


def loop(start, stop, body):
    def step(i, carry):
        body(jnp.int32(i))
        return carry

    lax.fori_loop(start, stop, step, 0)


def gather_kernel(n_row, n_col, mine, out, send, recv, near_send, near_recv):
    at = Place(n_row, n_col)
    barrier = pltpu.get_barrier_semaphore()
    loop(1, at.chips, lambda k: signal(barrier, at.at(row=at.chip(k) * 2 + at.core)))
    signal(barrier, at.sibling())
    pl.semaphore_wait(barrier, at.chips)

    def far(k):
        return remote(mine, out.at[at.row], send.at[k], recv.at[k], at.at(row=at.chip(k) * 2 + at.core))

    def near(k):
        held = out.at[at.chip(k, -1) * 2 + at.core]
        return remote(held, held, near_send.at[k], near_recv.at[k], at.sibling())

    loop(1, at.chips, lambda k: far(k).start())
    out[at.row] = mine[...]
    near(jnp.int32(0)).start()

    def pass_on(k):
        far(k).wait_recv()
        near(k).start()

    loop(1, at.chips, pass_on)
    loop(1, at.chips, lambda k: far(k).wait_send())
    loop(0, at.chips, lambda k: near(k).wait())


def gather_rows(mine, n_row, n_col):
    chips = n_row // 2
    return pl.pallas_call(
        functools.partial(gather_kernel, n_row, n_col),
        out_shape=jax.ShapeDtypeStruct((n_row, *mine.shape), mine.dtype),
        in_specs=[pl.BlockSpec(memory_space=pltpu.VMEM)],
        out_specs=pl.BlockSpec(memory_space=pltpu.VMEM),
        scratch_shapes=[DMA((chips,))] * 4,
        compiler_params=pltpu.CompilerParams(
            collective_id=0, has_side_effects=True, vmem_limit_bytes=VMEM_LIMIT
        ),
        name="gather_rows",
    )(mine)


def product_kernel(backward, rows, cols, count, adj, panels, out, acc):
    acc[...] = jnp.zeros_like(acc)
    live = count[0]

    def product(b):
        if backward:
            value = jnp.dot(panels[rows[b]], adj[b], preferred_element_type=F32)
            return cols[b], value
        panel = panels[:, pl.ds(pl.multiple_of(cols[b] * adj.shape[2], adj.shape[2]), adj.shape[2])]
        return rows[b], lax.dot_general(adj[b], panel, NT, preferred_element_type=F32)

    def several(n, first):
        made = [product(first + i) for i in range(n)]
        for where, value in made:
            acc[where] += value

    turns = lax.div(live, 4)
    loop(0, turns, lambda t: several(4, t * 4))
    loop(turns * 4, live, lambda b: several(1, b))
    if backward:
        width = adj.shape[2]
        for c in range(acc.shape[0]):
            out[:, c * width : (c + 1) * width] = acc[c].astype(out.dtype)
    else:
        out[...] = acc[...].astype(out.dtype)


def block_product(adj, rows, cols, count, panels, blocks, backward):
    size = adj.shape[1]
    if backward:
        features = panels.shape[1]
        shape, acc = (features, blocks * size), (blocks, features, size)
    else:
        features = panels.shape[0]
        shape = acc = (blocks, size, features)
    smem, vmem = pl.BlockSpec(memory_space=pltpu.SMEM), pl.BlockSpec(memory_space=pltpu.VMEM)
    return pl.pallas_call(
        functools.partial(product_kernel, backward),
        out_shape=jax.ShapeDtypeStruct(shape, BF16),
        in_specs=[smem, smem, smem, vmem, vmem],
        out_specs=vmem,
        scratch_shapes=[pltpu.VMEM(acc, F32)],
        compiler_params=pltpu.CompilerParams(vmem_limit_bytes=VMEM_LIMIT),
        name="product_back" if backward else "product",
    )(rows, cols, count, adj, panels)


def lanes_of(n):
    return [
        (2 * way + half, 1 - 2 * way, half, n // 2 if way == half else (n - 1) // 2)
        for half in range(2)
        for way in range(2)
    ]


def middle_kernel(
    n_row, n_col, part, weight, cot, output, back, gw_part,
    ring, local, arrived, rs_send, rs_recv, ag_send, ag_recv, gw_send, gw_recv,
):
    at = Place(n_row, n_col)
    lanes = lanes_of(n_col)
    me = at.col
    most = max(steps for *_, steps in lanes)
    barrier = pltpu.get_barrier_semaphore()
    ways = [k for k in (1, n_col - 1)][: min(2, n_col - 1)]
    for k in ways:
        signal(barrier, at.at(col=at.peer_col(k)))
    loop(1, n_row, lambda k: signal(barrier, at.at(row=at.peer_row(k))))
    pl.semaphore_wait(barrier, len(ways) + n_row - 1)

    half_rows = part.shape[1] // 2

    def rs(lane, sign, s, src):
        return remote(src, ring.at[lane, s], rs_send.at[lane, s], rs_recv.at[lane, s], at.at(col=at.peer_col(sign)))

    def addend(sign, half, steps, s):
        return part.at[at.peer_col(sign * (steps - s)), pl.ds(half * half_rows, half_rows)]

    for lane, sign, half, steps in lanes:
        if steps:
            rs(lane, sign, 0, addend(sign, half, steps, 0)).start()

    def rs_step(s):
        for lane, sign, half, steps in lanes:

            @pl.when(s < steps)
            def _():
                rs(lane, sign, s - 1, ring.at[lane, s - 1]).wait_recv()
                total = ring[lane, s - 1].astype(F32) + addend(sign, half, steps, s)[...].astype(F32)
                ring[lane, s - 1] = total.astype(BF16)
                rs(lane, sign, s, ring.at[lane, s - 1]).start()

    loop(1, most, rs_step)
    halves = [part[me, h * half_rows : (h + 1) * half_rows].astype(F32) for h in range(2)]
    for lane, sign, half, steps in lanes:
        if steps:
            rs(lane, sign, steps - 1, ring.at[lane, steps - 1]).wait_recv()
            halves[half] += ring[lane, steps - 1].astype(F32)
    aggregated = jnp.concatenate(halves, axis=0).astype(BF16)

    preact = jnp.dot(aggregated, weight[...], preferred_element_type=F32)
    sigmoid = jax.nn.sigmoid(preact)
    slopes = sigmoid * (1.0 + preact * (1.0 - sigmoid))
    deltas = (cot[...].astype(F32) * slopes).astype(BF16)
    back[me] = lax.dot_general(weight[...], deltas, NT, preferred_element_type=F32).astype(BF16)

    half_back = back.shape[1] // 2

    def ag(lane, sign, half, s):
        held = back.at[at.peer_col(-sign * s), pl.ds(half * half_back, half_back)]
        return remote(held, held, ag_send.at[lane, s], ag_recv.at[lane, s], at.at(col=at.peer_col(sign)))

    def ag_wait(lane, sign, half, s):
        held = back.at[at.peer_col(-sign * (s + 1)), pl.ds(half * half_back, half_back)]
        remote(held, held, ag_send.at[lane, s], ag_recv.at[lane, s], at.at(col=at.peer_col(sign))).wait_recv()

    for lane, sign, half, steps in lanes:
        if steps:
            ag(lane, sign, half, 0).start()

    output[...] = (preact * sigmoid).astype(BF16)
    grad = lax.dot_general(aggregated, deltas, TN, preferred_element_type=F32)
    local[...] = grad.reshape(local.shape)

    def gw(k):
        return remote(local.at[at.peer_row(k)], arrived.at[k - 1], gw_send.at[k - 1], gw_recv, at.at(row=at.peer_row(k)))

    loop(1, n_row, lambda k: gw(k).start())

    def ag_step(s):
        for lane, sign, half, steps in lanes:

            @pl.when(s < steps)
            def _():
                ag_wait(lane, sign, half, s - 1)
                ag(lane, sign, half, s).start()

    loop(1, most, ag_step)
    remote(arrived, arrived, gw_send.at[0], gw_recv, at.sibling()).wait_recv()
    total = local[at.row]
    for k in range(n_row - 1):
        total += arrived[k]
    gw_part[...] = total
    for lane, sign, half, steps in lanes:
        if steps:
            ag_wait(lane, sign, half, steps - 1)
    loop(1, n_row, lambda k: gw(k).wait_send())

    def drain(s):
        for lane, sign, half, steps in lanes:

            @pl.when(s < steps)
            def _():
                rs(lane, sign, s, ring.at[lane, s]).wait_send()
                ag(lane, sign, half, s).wait_send()

    loop(0, most, drain)


def middle(part, weight, cot, n_row, n_col):
    blocks, size, features = part.shape
    steps = max(n_col // 2, 1)
    vmem = pl.BlockSpec(memory_space=pltpu.VMEM)
    ring_sems = DMA((4, steps))
    return pl.pallas_call(
        functools.partial(middle_kernel, n_row, n_col),
        out_shape=(
            jax.ShapeDtypeStruct((size, features), BF16),
            jax.ShapeDtypeStruct((blocks, features, size), BF16),
            jax.ShapeDtypeStruct((features // n_row, features), F32),
        ),
        in_specs=[vmem] * 3,
        out_specs=(vmem,) * 3,
        scratch_shapes=[
            pltpu.VMEM((4, steps, size // 2, features), BF16),
            pltpu.VMEM((n_row, features // n_row, features), F32),
            pltpu.VMEM((n_row - 1, features // n_row, features), F32),
            ring_sems, ring_sems, ring_sems, ring_sems,
            DMA((n_row - 1,)),
            DMA(()),
        ],
        compiler_params=pltpu.CompilerParams(
            collective_id=1, has_side_effects=True, vmem_limit_bytes=VMEM_LIMIT
        ),
        name="middle",
    )(part, weight, cot)


def final_kernel(
    n_row, n_col, scale, terms, gw_part, grad, gw,
    swapped, staged, arrived, z_buf, x_send, x_recv, f_send, f_recv, z_send, z_recv, g_send, g_recv,
):
    at = Place(n_row, n_col)
    barrier = pltpu.get_barrier_semaphore()
    loop(1, n_row, lambda k: signal(barrier, at.at(row=at.peer_row(k))))
    loop(1, n_col, lambda k: signal(barrier, at.at(col=at.peer_col(k))))
    pl.semaphore_wait(barrier, n_row + n_col - 2)

    def swap(k):
        return remote(terms.at[at.chip(k), 1 - at.core], swapped.at[k], x_send.at[k], x_recv.at[k], at.sibling())

    def far(k):
        return remote(
            staged.at[k], arrived.at[k - 1], f_send.at[k], f_recv.at[k], at.at(row=at.chip(k) * 2 + at.core)
        )

    def z_copy(k):
        return remote(gw_part, z_buf.at[at.col], z_send.at[k], z_recv, at.at(col=at.peer_col(k)))

    def g_copy(k):
        return remote(gw.at[at.row], gw.at[at.row], g_send.at[k], g_recv, at.at(row=at.peer_row(k)))

    loop(0, at.chips, lambda k: swap(lax.rem(k + 1, at.chips)).start())
    loop(1, n_col, lambda k: z_copy(k).start())
    z_buf[at.col] = gw_part[...]

    def add(k):
        swap(k).wait_recv()
        return terms[at.chip(k), at.core].astype(F32) + swapped[k].astype(F32)

    def add_and_send(k):
        staged[k] = add(k).astype(BF16)
        far(k).start()

    loop(1, at.chips, add_and_send)
    total = add(jnp.int32(0))
    if n_col > 1:
        most = z_buf.at[pl.ds(0, n_col - 1)]
        remote(most, most, z_send.at[0], z_recv, at.sibling()).wait_recv()
    whole = z_buf[0]
    for k in range(1, n_col):
        whole += z_buf[k]
    gw[at.row] = whole * scale
    loop(1, n_row, lambda k: g_copy(k).start())
    for k in range(1, at.chips):
        far(jnp.int32(k)).wait_recv()
        total += arrived[k - 1].astype(F32)
    grad[...] = total.astype(BF16)
    rest = gw.at[pl.ds(0, n_row - 1)]
    remote(rest, rest, g_send.at[0], g_recv, at.sibling()).wait_recv()
    loop(0, at.chips, lambda k: swap(k).wait_send())
    loop(1, at.chips, lambda k: far(k).wait_send())
    loop(1, n_col, lambda k: z_copy(k).wait_send())
    loop(1, n_row, lambda k: g_copy(k).wait_send())


def final(terms, gw_part, n_row, n_col, scale):
    chips, _, some, nodes = terms.shape
    vmem = pl.BlockSpec(memory_space=pltpu.VMEM)
    return pl.pallas_call(
        functools.partial(final_kernel, n_row, n_col, scale),
        out_shape=(
            jax.ShapeDtypeStruct((some, nodes), BF16),
            jax.ShapeDtypeStruct((n_row, *gw_part.shape), F32),
        ),
        in_specs=[vmem] * 2,
        out_specs=(vmem,) * 2,
        scratch_shapes=[
            pltpu.VMEM((chips, some, nodes), BF16),
            pltpu.VMEM((chips, some, nodes), BF16),
            pltpu.VMEM((max(chips - 1, 1), some, nodes), BF16),
            pltpu.VMEM((n_col, *gw_part.shape), F32),
            DMA((chips,)), DMA((chips,)), DMA((chips,)), DMA((chips,)),
            DMA((n_col,)), DMA(()), DMA((n_row,)), DMA(()),
        ],
        compiler_params=pltpu.CompilerParams(
            collective_id=2, has_side_effects=True, vmem_limit_bytes=VMEM_LIMIT
        ),
        name="final",
    )(terms, gw_part)


def solution(mesh):
    n_row, n_col = mesh.shape["row"], mesh.shape["col"]

    def shards(features, weight, adj_values, block_rows, block_cols, block_counts, cotangent):
        adj, rows, cols, count = adj_values[0, 0], block_rows[0, 0], block_cols[0, 0], block_counts[0]
        size = adj.shape[1]
        nodes = features.shape[0]
        width = weight.shape[0]
        panels = gather_rows(features.T, n_row, n_col).reshape(width, nodes)
        part = block_product(adj, rows, cols, count, panels, n_col, False)
        output, back, gw_part = middle(part, weight, cotangent, n_row, n_col)
        terms = block_product(adj, rows, cols, count, back, nodes // size, True)
        terms = terms.reshape(n_row // 2, 2, width // n_row, nodes)
        grad, gw = final(terms, gw_part, n_row, n_col, 1.0 / math.sqrt(nodes * n_col))
        return output, gw.reshape(width, width), grad.T

    return jax.shard_map(
        shards,
        mesh=mesh,
        in_specs=(
            P("col", "row"),
            P(),
            P("row", "col", None, None, None),
            P("row", "col", None),
            P("row", "col", None),
            P("row", "col"),
            P(("row", "col"), None),
        ),
        out_specs=(P(("row", "col"), None), P(), P("col", "row")),
        check_vma=False,
    )
```

time: 849 us -> 148 us (0.17)
  waiting for transfers between devices: 737 us -> 0 us
  Pallas kernels: 0 us -> 143 us
  other arithmetic: 49 us -> 0 us
  local copies, waits for them, and re-layouts: 30 us -> 3.78 us
  matrix products: 15.8 us -> 0 us
  between operations: 14.5 us -> 1.31 us
    psum x1 -> x0, waiting for transfers between devices: 426 us -> none  [shards(): lax.psum(local_grad, ('row', 'col')) * (1.0 / math.sqrt(node_total))]
    reduce_scatter x2 -> x0, waiting for transfers between devices: 177 us -> none  [the longest x1 101 us: shards(): lax.psum_scatter(column_terms.astype(jnp.bfloat16), 'row', scatter_dimens...]
    pallas_call x0 -> x5, Pallas kernels: none -> 143 us  [the longest x1 61.9 us: middle(): pl.pallas_call(functools.partial(middle_kernel, n_row, n_col), out_shape=...]
    all_gather x2 -> x0, waiting for transfers between devices: 133 us -> none  [the longest x1 67.4 us: shards(): panel_part = lax.all_gather(features, 'row', axis=1, tiled=True)]
    scatter-add x8 -> x0, other arithmetic: 35.5 us -> none  [step(): return running.at[target_ids].add(contribution)]
    gather x8 -> x0, local copies, waits for them, and re-layouts: 16.2 us -> none  [the longest x4 8.82 us: step(): picked = jnp.take(panels, col_ids, axis=0)]
    dot_general x11 -> x0, matrix products: 15.8 us -> none  [the longest x4 6.2 us: step(): jnp.einsum('bij,bif->bjf', values_now, picked, preferred_element_type=jnp...]
  transfers between devices with their start and end apart: 5 -> 0, of which waited for: 5 -> 0; matrix products, arithmetic and copies ran while one was open for 6% -> 0% of each run, Pallas kernels for 0% -> 0%
where the time goes in v1:
time: 148 us
  Pallas kernels  143 us (97%)
  local copies, waits for them, and re-layouts  3.78 us (3%)
    pallas_call x1, Pallas kernels, middle(): pl.pallas_call(functools.partial(middle_kernel, n_row, n_col), out_shape=...  61.9 us
    pallas_call x1, Pallas kernels, final(): pl.pallas_call(functools.partial(final_kernel, n_row, n_col, scale), out_...  42.8 us
    pallas_call x1, Pallas kernels, gather_rows(): pl.pallas_call(functools.partial(gather_kernel, n_row, n_col), out_shape=...  25.8 us
    pallas_call x2, Pallas kernels, block_product(): pl.pallas_call(functools.partial(product_kernel, backward), out_shape=jax...  12.4 us
    unnamed x5, local copies, waits for them, and re-layouts  3.78 us

profile of v1, /device:TPU:1, one launch (start us, length us, event | category | flops | bytes accessed | tf_op | source)
XLA Modules:
  0.0 148.0 jit_solution(6745342012624774980)
XLA Ops:
  1.3 25.8 %gather_rows.1 = bf16[32,8,4096]{2,1,0:T(8,128)(2,1)} custom-call(bf16[8,4096]{1,0:T(8,128)(2,1)} %bitcast.16), custom_call_target="tpu_custom_call" | custom-call | tf_op jit(solution)/shard_map/gather_rows/pallas_call | solution.py:95
  27.1 6.1 %product.1.part = bf16[16,128,256]{2,1,0:T(8,128)(2,1)} custom-call(s32[96]{0:T(128)} %bitcast.18, s32[96]{0:T(128)} %bitcast.20, s32[1]{0:T(128)} %bitcast.9.count, bf16[96,128,128]{2,1,0:T(8,128)(2,1)} %bitcast.11, bf16[256,4096]{1,0:T(8,128)(2,1)} %bitcast.14), custom_call_target="tpu_custom_call" | custom-call | tf_op jit(solution)/shard_map/product/pallas_call | solution.py:144
  33.1 61.9 %middle.1 = (bf16[128,256]{1,0:T(8,128)(2,1)}, bf16[16,256,128]{2,1,0:T(8,128)(2,1)}, f32[8,256]{1,0:T(8,128)}) custom-call(bf16[16,128,256]{2,1,0:T(8,128)(2,1)} %product.1.part, bf16[256,256]{1,0:T(8,128)(2,1)} %weight.1, bf16[128,256]{1,0:T(8,128)(2,1)} %cot.1), custom_call_target="tpu_custom_call" | custom-call | tf_op jit(solution)/shard_map/middle/pallas_call | solution.py:272
  95.0 6.4 %product_back.1 = bf16[256,4096]{1,0:T(8,128)(2,1)} custom-call(s32[96]{0:T(128)} %bitcast.19, s32[96]{0:T(128)} %bitcast.21, s32[1]{0:T(128)} %bitcast.10.count, bf16[96,128,128]{2,1,0:T(8,128)(2,1)} %bitcast.12, bf16[16,256,128]{2,1,0:T(8,128)(2,1)} %get-tuple-element.9.panels), custom_call_target="tpu_custom_call" | custom-call | tf_op jit(solution)/shard_map/product_back/pallas_call | solution.py:144
  101.4 0.0 copy-start
  101.4 42.8 %final.1 = (bf16[8,4096]{1,0:T(8,128)(2,1)}, f32[32,8,256]{2,1,0:T(8,128)}) custom-call(bf16[16,2,8,4096]{3,2,1,0:T(8,128)(2,1)} %bitcast.13, f32[8,256]{1,0:T(8,128)} %get-tuple-element.10.gw_part), custom_call_target="tpu_custom_call" | custom-call | tf_op jit(solution)/shard_map/final/pallas_call | solution.py:357
  144.2 0.0 copy-done
  144.2 0.6 copy.14
  144.8 1.7 %copy.15 = f32[256,256]{1,0:T(8,128)} copy(f32[256,256]{1,0:T(8,128)} %bitcast.15) | data formatting | bytes 524288
  146.5 1.5 copy.16
Async XLA Ops:
  101.4 42.8 %copy-start = (bf16[128,256]{1,0:T(8,128)(2,1)S(1)}, bf16[128,256]{1,0:T(8,128)(2,1)}, u32[]{:S(2)}) copy-start(bf16[128,256]{1,0:T(8,128)(2,1)} %get-tuple-element.16) | copy-start | bytes 196612

commit v2 on v0

v2 whole, which is shorter than its diff:
```python
import functools
import math

import jax
import jax.numpy as jnp
from jax import lax
from jax.experimental import pallas as pl
from jax.experimental.pallas import tpu as pltpu
from jax.sharding import PartitionSpec as P

MESH = pl.DeviceIdType.MESH
VMEM_LIMIT = 56 * 2**20
NT = (((1,), (1,)), ((), ()))
TN = (((0,), (0,)), ((), ()))
DMA = pltpu.SemaphoreType.DMA
BF16, F32 = jnp.bfloat16, jnp.float32


class Place:
    def __init__(self, n_row, n_col):
        self.n_row, self.n_col = n_row, n_col
        self.chips = n_row // 2
        self.side = math.isqrt(self.chips)
        self.row, self.col = lax.axis_index("row"), lax.axis_index("col")
        self.core = lax.rem(self.row, 2)
        chip = lax.div(self.row, 2)
        self.x, self.y = lax.div(chip, self.side), lax.rem(chip, self.side)

    def chip(self, k, sign=1):
        dx, dy = lax.div(k, self.side), lax.rem(k, self.side)
        x = lax.rem(self.x + sign * dx + self.side, self.side)
        y = lax.rem(self.y + sign * dy + self.side, self.side)
        return x * self.side + y

    def at(self, row=None, col=None):
        return (self.row if row is None else row, self.col if col is None else col)

    def sibling(self):
        return self.at(row=self.row + 1 - 2 * self.core)

    def peer_row(self, k):
        return lax.rem(self.row + k, self.n_row)

    def peer_col(self, k):
        return lax.rem(self.col + k + self.n_col, self.n_col)


def signal(barrier, device):
    pl.semaphore_signal(barrier, inc=1, device_id=device, device_id_type=MESH)


def remote(src, dst, send, recv, device):
    return pltpu.make_async_remote_copy(
        src_ref=src, dst_ref=dst, send_sem=send, recv_sem=recv, device_id=device, device_id_type=MESH
    )


def loop(start, stop, body):
    def step(i, carry):
        body(jnp.int32(i))
        return carry

    lax.fori_loop(start, stop, step, 0)


def lanes_of():
    return [(2 * way + half, 1 - 2 * way, half, way == half) for half in range(2) for way in range(2)]


def whole_kernel(
    n_row, n_col, scale,
    idx, mine, weight, cot, adj_hbm,
    output, gw, grad,
    adj, gathered, panels, part, chain, side, back, acc, terms, swapped, staged, arrived,
    g_local, g_swap, g_sum, g_arrived, z_buf,
    adj_sem, f_send, f_recv, n_send, n_recv, rc_send, rc_recv, rs_send, rs_recv, ac_send, ac_recv, as_send, as_recv,
    gx_send, gx_recv, gp_send, gp_recv, gz_send, gz_recv, go_send, go_recv, gy_send, gy_recv,
    x_send, x_recv, p_send, p_recv,
):
    at = Place(n_row, n_col)
    lanes = lanes_of()
    me, chips = at.col, at.chips
    my_chip = lax.div(at.row, 2)
    slots, size = adj_hbm.shape[0], adj_hbm.shape[1]
    blocks = acc.shape[0] * 2
    width = weight.shape[0]

    load_adj = pltpu.make_async_copy(adj_hbm, adj.at[pl.ds(0, slots)], adj_sem)
    load_adj.start()

    barrier = pltpu.get_barrier_semaphore()
    loop(1, chips, lambda k: signal(barrier, at.at(row=at.chip(k) * 2 + at.core)))
    signal(barrier, at.sibling())
    loop(1, n_col, lambda k: signal(barrier, at.at(col=at.peer_col(k))))
    adj[slots] = jnp.zeros((size, size), BF16)
    pl.semaphore_wait(barrier, chips + n_col - 1)

    def same_core(k):
        return at.at(row=at.chip(k) * 2 + at.core)

    def far(k):
        return remote(mine, gathered.at[at.row], f_send.at[k], f_recv.at[k], same_core(k))

    def near(k):
        held = gathered.at[at.chip(k, -1) * 2 + at.core]
        return remote(held, held, n_send.at[k], n_recv.at[k], at.sibling())

    loop(1, chips, lambda k: far(k).start())
    gathered[at.row] = mine[...]
    near(jnp.int32(0)).start()

    def pass_on(k):
        far(k).wait_recv()
        near(k).start()

    loop(1, chips, pass_on)
    load_adj.wait()
    loop(0, chips, lambda k: near(k).wait_recv())
    panels[...] = gathered[...].reshape(panels.shape)

    def row_of(r):
        return jnp.concatenate([adj[idx[r * blocks + c]] for c in range(blocks)], axis=1)

    def aggregate(a, b):
        both = jnp.concatenate([row_of(a), row_of(b)], axis=0)
        made = lax.dot_general(both, panels[...], NT, preferred_element_type=F32).astype(BF16)
        part[a] = made[:size]
        part[b] = made[size:]

    def aggregate_first(i):
        a = at.peer_col(8 - i)
        aggregate(a, at.peer_col(-7 * i))

    loop(0, 2, aggregate_first)

    half_rows = size // 2

    def piece(k, half):
        return part.at[at.peer_col(k), pl.ds(half * half_rows, half_rows)]

    def rc(lane, sign, t, src):
        return remote(src, chain.at[lane, t], rc_send.at[lane, t], rc_recv.at[lane, t], at.at(col=at.peer_col(2 * sign)))

    def rs(lane, sign, half, t):
        src = piece(sign * (7 - 2 * t), half)
        return remote(src, side.at[lane, t], rs_send.at[lane, t], rs_recv.at[lane, t], at.at(col=at.peer_col(sign)))

    for lane, sign, half, long in lanes:
        if long:
            rc(lane, sign, 0, piece(8 * sign, half)).start()
    for lane, sign, half, long in lanes:
        rs(lane, sign, half, 0).start()

    def rs_step(t):
        loop(0, 2, lambda i: aggregate(at.peer_col(8 - 2 * t - i), at.peer_col(2 * t + i - 8)))
        for lane, sign, half, long in lanes:
            total = piece(sign * (8 - 2 * t), half)[...].astype(F32)
            rs(lane, sign, half, t - 1).wait_recv()
            total += side[lane, t - 1].astype(F32)
            if long:
                rc(lane, sign, t - 1, chain.at[lane, t - 1]).wait_recv()
                total += chain[lane, t - 1].astype(F32)
                chain[lane, t - 1] = total.astype(BF16)
            else:

                @pl.when(t > 1)
                def _():
                    rc(lane, sign, t - 1, chain.at[lane, t - 1]).wait_recv()
                    chain[lane, t - 1] = (total + chain[lane, t - 1].astype(F32)).astype(BF16)

                @pl.when(t == 1)
                def _():
                    chain[lane, 0] = total.astype(BF16)

            rc(lane, sign, t, chain.at[lane, t - 1]).start()
            rs(lane, sign, half, t).start()

    loop(1, 4, rs_step)
    halves = [part[me, h * half_rows : (h + 1) * half_rows].astype(F32) for h in range(2)]
    for lane, sign, half, long in lanes:
        rs(lane, sign, half, 3).wait_recv()
        rc(lane, sign, 3, chain.at[lane, 3]).wait_recv()
        halves[half] += side[lane, 3].astype(F32) + chain[lane, 3].astype(F32)
    aggregated = jnp.concatenate(halves, axis=0).astype(BF16)

    preact = jnp.dot(aggregated, weight[...], preferred_element_type=F32)
    sigmoid = jax.nn.sigmoid(preact)
    slopes = sigmoid * (1.0 + preact * (1.0 - sigmoid))
    deltas = (cot[...].astype(F32) * slopes).astype(BF16)
    back[me] = lax.dot_general(weight[...], deltas, NT, preferred_element_type=F32).astype(BF16)

    half_back = width // 2

    def held(k, half):
        return back.at[at.peer_col(k), pl.ds(half * half_back, half_back)]

    def ac(lane, sign, half, t):
        ref = held(-2 * sign * t, half)
        return remote(ref, ref, ac_send.at[lane, t], ac_recv.at[lane, t], at.at(col=at.peer_col(2 * sign)))

    def ac_wait(lane, sign, half, t):
        ref = held(-2 * sign * (t + 1), half)
        remote(ref, ref, ac_send.at[lane, t], ac_recv.at[lane, t], at.at(col=at.peer_col(2 * sign))).wait_recv()

    def as_(lane, sign, half, t):
        ref = held(-2 * sign * t, half)
        return remote(ref, ref, as_send.at[lane, t], as_recv.at[lane, t], at.at(col=at.peer_col(sign)))

    def as_wait(lane, sign, half, t):
        ref = held(-sign * (2 * t + 1), half)
        remote(ref, ref, as_send.at[lane, t], as_recv.at[lane, t], at.at(col=at.peer_col(sign))).wait_recv()

    for lane, sign, half, long in lanes:
        ac(lane, sign, half, 0).start()
    for lane, sign, half, long in lanes:
        as_(lane, sign, half, 0).start()

    def columns(rows, q):
        return jnp.concatenate(
            [jnp.concatenate([adj[idx[r * blocks + 2 * q + i]] for i in range(2)], axis=1) for r in rows], axis=0
        )

    def spread(rows):
        lhs = jnp.concatenate([back[r] for r in rows], axis=1)
        return lambda q: jnp.dot(lhs, columns(rows, q), preferred_element_type=F32)

    output[...] = (preact * sigmoid).astype(BF16)
    g_local[...] = lax.dot_general(aggregated, deltas, TN, preferred_element_type=F32).reshape(g_local.shape)
    g_x = remote(g_local.at[:, 1 - at.core], g_swap, gx_send, gx_recv, at.sibling())
    g_x.start()
    own = spread([me])
    for q in range(blocks // 2):
        acc[q] = own(q)

    def g_p(k):
        return remote(g_sum.at[at.chip(k)], g_arrived.at[k - 1], gp_send.at[k], gp_recv, same_core(k))

    g_x.wait_recv()
    g_sum[...] = g_local[:, at.core] + g_swap[...]
    loop(1, chips, lambda k: g_p(k).start())

    def ag_step(t):
        for lane, sign, half, long in lanes:
            ac_wait(lane, sign, half, t - 1)
            if long:
                ac(lane, sign, half, t).start()
            else:
                pl.when(t < 3)(lambda: ac(lane, sign, half, t).start())
            as_(lane, sign, half, t).start()
        for lane, sign, half, long in lanes:
            as_wait(lane, sign, half, t - 1)

        def pair(i):
            k = 2 * t - 1 + i
            made = spread([at.peer_col(k), at.peer_col(-k)])
            for q in range(blocks // 2):
                acc[q] += made(q)

        loop(0, 2, pair)

    loop(1, 4, ag_step)

    if chips > 1:
        remote(g_arrived, g_arrived, gp_send.at[0], gp_recv, at.sibling()).wait_recv()
    total = g_sum[my_chip]
    for k in range(chips - 1):
        total += g_arrived[k]
    z_buf[me] = total

    def g_z(k):
        return remote(z_buf.at[me], z_buf.at[me], gz_send.at[k], gz_recv, at.at(col=at.peer_col(k)))

    loop(1, n_col, lambda k: g_z(k).start())

    for lane, sign, half, long in lanes:
        as_wait(lane, sign, half, 3)
    for lane, sign, half, long in lanes:
        if long:
            ac_wait(lane, sign, half, 3)

    nodes = terms.shape[3] // 2

    def swap(h):
        return remote(
            terms.at[:, 1 - at.core, :, pl.ds(h * nodes, nodes)], swapped.at[h], x_send.at[h], x_recv.at[h], at.sibling()
        )

    last = spread([at.peer_col(7), at.peer_col(-7), at.peer_col(8)])
    for q in range(blocks // 2):
        made = (acc[q] + last(q)).astype(BF16)
        terms[:, :, :, q * 2 * size : (q + 1) * 2 * size] = made.reshape(*terms.shape[:3], 2 * size)
        if (q + 1) % (blocks // 4) == 0:
            swap((q + 1) // (blocks // 4) - 1).start()

    def term(c, h):
        return terms[c, at.core, :, h * nodes : (h + 1) * nodes].astype(F32) + swapped[h, c].astype(F32)

    def plane(k, h):
        return remote(
            staged.at[h, at.chip(k)], arrived.at[h, k - 1], p_send.at[h, k], p_recv.at[h, k], same_core(k)
        )

    sums = []
    for h in range(2):
        swap(h).wait_recv()

        def add_and_send(k):
            staged[h, at.chip(k)] = term(at.chip(k), h).astype(BF16)
            plane(k, h).start()

        loop(1, chips, add_and_send)
        sums.append(term(my_chip, h))

    most = z_buf.at[pl.ds(0, n_col - 1)]
    remote(most, most, gz_send.at[0], gz_recv, at.sibling()).wait_recv()
    whole = z_buf[0]
    for k in range(1, n_col):
        whole += z_buf[k]
    gw[my_chip, at.core] = whole * scale

    def g_o(k):
        ref = gw.at[my_chip, at.core]
        return remote(ref, ref, go_send.at[k], go_recv, same_core(k))

    loop(1, chips, lambda k: g_o(k).start())
    if chips > 1:
        rest = gw.at[pl.ds(0, chips - 1), at.core]
        remote(rest, rest, go_send.at[0], go_recv, at.sibling()).wait_recv()
    g_y = remote(gw.at[:, at.core], gw.at[:, at.core], gy_send, gy_recv, at.sibling())
    g_y.start()

    for h in range(2):
        for k in range(1, chips):
            plane(jnp.int32(k), h).wait_recv()
            sums[h] += arrived[h, k - 1].astype(F32)
        grad[:, h * nodes : (h + 1) * nodes] = sums[h].astype(BF16)
    g_y.wait()

    g_x.wait_send()
    loop(0, chips, lambda k: near(k).wait_send())

    def drain(k):
        far(k).wait_send()
        g_p(k).wait_send()
        g_o(k).wait_send()
        for h in range(2):
            plane(k, h).wait_send()

    loop(1, chips, drain)
    loop(1, n_col, lambda k: g_z(k).wait_send())
    for h in range(2):
        swap(h).wait_send()

    for lane, sign, half, long in lanes:

        def drain_lane(t):
            rs(lane, sign, half, t).wait_send()
            as_(lane, sign, half, t).wait_send()

        loop(0, 4, drain_lane)
        loop(0 if long else 1, 4, lambda t: rc(lane, sign, t, chain.at[lane, t]).wait_send())
        loop(0, 4 if long else 3, lambda t: ac(lane, sign, half, t).wait_send())


def whole(idx, mine, weight, cot, adj, n_row, n_col, scale):
    some, nodes = mine.shape
    slots, size, _ = adj.shape
    width = weight.shape[0]
    chips = n_row // 2
    assert n_col == 16 and nodes % (2 * size) == 0
    vmem = pl.BlockSpec(memory_space=pltpu.VMEM)
    V = pltpu.VMEM
    few = max(chips - 1, 1)
    return pl.pallas_call(
        functools.partial(whole_kernel, n_row, n_col, scale),
        out_shape=(
            jax.ShapeDtypeStruct((size, width), BF16),
            jax.ShapeDtypeStruct((chips, 2, some, width), F32),
            jax.ShapeDtypeStruct((some, nodes), BF16),
        ),
        in_specs=[pl.BlockSpec(memory_space=pltpu.SMEM), vmem, vmem, vmem, pl.BlockSpec(memory_space=pl.ANY)],
        out_specs=(vmem,) * 3,
        scratch_shapes=[
            V((slots + 1, size, size), BF16),
            V((n_row, some, nodes), BF16),
            V((width, nodes), BF16),
            V((n_col, size, width), BF16),
            V((4, 4, size // 2, width), BF16),
            V((4, 4, size // 2, width), BF16),
            V((n_col, width, size), BF16),
            V((nodes // (2 * size), width, 2 * size), F32),
            V((chips, 2, some, nodes), BF16),
            V((2, chips, some, nodes // 2), BF16),
            V((2, chips, some, nodes // 2), BF16),
            V((2, few, some, nodes // 2), BF16),
            V((chips, 2, some, width), F32),
            V((chips, some, width), F32),
            V((chips, some, width), F32),
            V((few, some, width), F32),
            V((n_col, some, width), F32),
            DMA(()),
            *[DMA((chips,))] * 4,
            *[DMA((4, 4))] * 8,
            DMA(()), DMA(()),
            DMA((chips,)), DMA(()),
            DMA((n_col,)), DMA(()),
            DMA((chips,)), DMA(()),
            DMA(()), DMA(()),
            DMA((2,)), DMA((2,)),
            DMA((2, chips)), DMA((2, chips)),
        ],
        compiler_params=pltpu.CompilerParams(
            collective_id=0, has_side_effects=True, vmem_limit_bytes=VMEM_LIMIT
        ),
        name="whole",
    )(idx, mine, weight, cot, adj)


def block_table(rows, cols, count, n_rows, n_cols):
    slots = rows.shape[0]
    slot = jnp.arange(slots, dtype=jnp.int32)
    place = jnp.where(slot < count, rows * n_cols + cols, -1)
    here = place[:, None] == jnp.arange(n_rows * n_cols, dtype=jnp.int32)[None, :]
    return jnp.min(jnp.where(here, slot[:, None], slots), axis=0)


def solution(mesh):
    n_row, n_col = mesh.shape["row"], mesh.shape["col"]

    def shards(features, weight, adj_values, block_rows, block_cols, block_counts, cotangent):
        adj = adj_values[0, 0]
        nodes, width = features.shape[0], weight.shape[0]
        idx = block_table(block_rows[0, 0], block_cols[0, 0], block_counts[0, 0], n_col, nodes // adj.shape[1])
        scale = 1.0 / math.sqrt(nodes * n_col)
        output, gw, grad = whole(idx, features.T, weight, cotangent, adj, n_row, n_col, scale)
        return output, gw.reshape(width, width), grad.T

    return jax.shard_map(
        shards,
        mesh=mesh,
        in_specs=(
            P("col", "row"),
            P(),
            P("row", "col", None, None, None),
            P("row", "col", None),
            P("row", "col", None),
            P("row", "col"),
            P(("row", "col"), None),
        ),
        out_specs=(P(("row", "col"), None), P(), P("col", "row")),
        check_vma=False,
    )
```

time: 849 us -> 108 us (0.13)
  waiting for transfers between devices: 737 us -> 0 us
  Pallas kernels: 0 us -> 101 us
  other arithmetic: 49 us -> 1.36 us
  local copies, waits for them, and re-layouts: 30 us -> 4.61 us
  matrix products: 15.8 us -> 0 us
  between operations: 14.5 us -> 1.29 us
    psum x1 -> x0, waiting for transfers between devices: 426 us -> none  [shards(): lax.psum(local_grad, ('row', 'col')) * (1.0 / math.sqrt(node_total))]
    reduce_scatter x2 -> x0, waiting for transfers between devices: 177 us -> none  [the longest x1 101 us: shards(): lax.psum_scatter(column_terms.astype(jnp.bfloat16), 'row', scatter_dimens...]
    all_gather x2 -> x0, waiting for transfers between devices: 133 us -> none  [the longest x1 67.4 us: shards(): panel_part = lax.all_gather(features, 'row', axis=1, tiled=True)]
    pallas_call x0 -> x1, Pallas kernels: none -> 101 us  [whole(): pl.pallas_call(functools.partial(whole_kernel, n_row, n_col, scale), out_...]
    scatter-add x8 -> x0, other arithmetic: 35.5 us -> none  [step(): return running.at[target_ids].add(contribution)]
    gather x8 -> x0, local copies, waits for them, and re-layouts: 16.2 us -> none  [the longest x4 8.82 us: step(): picked = jnp.take(panels, col_ids, axis=0)]
    dot_general x11 -> x0, matrix products: 15.8 us -> none  [the longest x4 6.2 us: step(): jnp.einsum('bij,bif->bjf', values_now, picked, preferred_element_type=jnp...]
  transfers between devices with their start and end apart: 5 -> 0, of which waited for: 5 -> 0; matrix products, arithmetic and copies ran while one was open for 6% -> 0% of each run, Pallas kernels for 0% -> 0%
where the time goes in v2:
time: 108 us
  Pallas kernels  101 us (94%)
  local copies, waits for them, and re-layouts  4.61 us (4%)
  other arithmetic  1.36 us (1%)
  between operations  1.29 us (1%)
    pallas_call x1, Pallas kernels, whole(): pl.pallas_call(functools.partial(whole_kernel, n_row, n_col, scale), out_...  101 us
    unnamed x3, local copies, waits for them, and re-layouts  4.61 us

profile of v2, /device:TPU:1, one launch (start us, length us, event | category | flops | bytes accessed | tf_op | source)
XLA Modules:
  0.0 108.0 jit_solution(10746877517720917478)
XLA Ops:
  1.3 0.7 compare_select_fusion
  2.0 0.7 select_reduce_fusion.idx
  2.6 100.8 %whole.1 = (bf16[128,256]{1,0:T(8,128)(2,1)}, f32[16,2,8,256]{3,2,1,0:T(8,128)}, bf16[8,4096]{1,0:T(8,128)(2,1)}) custom-call(s32[512]{0:T(512)} %select_reduce_fusion.idx, bf16[8,4096]{1,0:T(8,128)(2,1)} %bitcast.10, bf16[256,256]{1,0:T(8,128)(2,1)} %weight.1, bf16[128,256]{1,0:T(8,128)(2,1)} %cot.1, bf16[96,128,128]{2,1,0:T(8,128)(2,1)} %bitcast.8), custom_call_target="tpu_custom_call" | custom-call | tf_op jit(solution)/shard_map/whole/pallas_call | solution.py:374
  103.4 1.5 %copy.14 = bf16[128,256]{1,0:T(8,128)(2,1)} copy(bf16[128,256]{1,0:T(8,128)(2,1)} %get-tuple-element.12) | data formatting | bytes 131072
  104.9 1.7 %copy.15 = f32[256,256]{1,0:T(8,128)} copy(f32[256,256]{1,0:T(8,128)} %bitcast.9) | data formatting | bytes 524288
  106.6 1.5 %copy.16 = bf16[4096,8]{0,1:T(8,128)(2,1)} copy(bf16[4096,8]{0,1:T(8,128)(2,1)} %bitcast.11) | data formatting | bytes 131072

commit v3 on v2

--- a/solution.py
+++ b/solution.py
@@ -69,12 +69,12 @@
 
 def whole_kernel(
     n_row, n_col, scale,
-    idx, mine, weight, cot, adj_hbm,
+    rows, cols, count, mine, weight_hbm, cot_hbm, adj_hbm,
     output, gw, grad,
-    adj, gathered, panels, part, chain, side, back, acc, terms, swapped, staged, arrived,
-    g_local, g_swap, g_sum, g_arrived, z_buf,
-    adj_sem, f_send, f_recv, n_send, n_recv, rc_send, rc_recv, rs_send, rs_recv, ac_send, ac_recv, as_send, as_recv,
-    gx_send, gx_recv, gp_send, gp_recv, gz_send, gz_recv, go_send, go_recv, gy_send, gy_recv,
+    table, idx, weight, cot, adj, gathered, panels, part, chain, side, back, acc, terms, swapped, staged, arrived,
+    g_local, g_swap, g_sum, g_arrived, z_near, z_far,
+    table_sem, weight_sem, cot_sem, adj_sem, f_send, f_recv, n_send, n_recv, rc_send, rc_recv, rs_send, rs_recv, ac_send, ac_recv, as_send, as_recv,
+    gx_send, gx_recv, gp_send, gp_recv, gz_send, gz_recv, gf_send, gf_recv, go_send, go_recv, gy_send, gy_recv,
     x_send, x_recv, p_send, p_recv,
 ):
     at = Place(n_row, n_col)
@@ -86,13 +86,29 @@
     width = weight.shape[0]
 
     load_adj = pltpu.make_async_copy(adj_hbm, adj.at[pl.ds(0, slots)], adj_sem)
+    load_weight = pltpu.make_async_copy(weight_hbm, weight, weight_sem)
+    load_cot = pltpu.make_async_copy(cot_hbm, cot, cot_sem)
     load_adj.start()
+    load_weight.start()
+    load_cot.start()
 
     barrier = pltpu.get_barrier_semaphore()
     loop(1, chips, lambda k: signal(barrier, at.at(row=at.chip(k) * 2 + at.core)))
     signal(barrier, at.sibling())
     loop(1, n_col, lambda k: signal(barrier, at.at(col=at.peer_col(k))))
     adj[slots] = jnp.zeros((size, size), BF16)
+
+    lanes_wide = table.shape[1]
+    position = lax.broadcasted_iota(jnp.int32, table.shape, 0) * lanes_wide + lax.broadcasted_iota(jnp.int32, table.shape, 1)
+    live = count[0]
+
+    def note_slot(s, held):
+        place = jnp.where(s < live, rows[s] * blocks + cols[s], -1)
+        return jnp.where(position == place, s, held)
+
+    table[...] = lax.fori_loop(0, slots, note_slot, jnp.full(table.shape, slots, jnp.int32))
+    load_table = pltpu.make_async_copy(table, idx, table_sem)
+    load_table.start()
     pl.semaphore_wait(barrier, chips + n_col - 1)
 
     def same_core(k):
@@ -115,11 +131,17 @@
 
     loop(1, chips, pass_on)
     load_adj.wait()
+    load_table.wait()
     loop(0, chips, lambda k: near(k).wait_recv())
     panels[...] = gathered[...].reshape(panels.shape)
 
+    per_line = lanes_wide // blocks
+
+    def block(r, c):
+        return adj[idx[lax.div(r, per_line), lax.rem(r, per_line) * blocks + c]]
+
     def row_of(r):
-        return jnp.concatenate([adj[idx[r * blocks + c]] for c in range(blocks)], axis=1)
+        return jnp.concatenate([block(r, c) for c in range(blocks)], axis=1)
 
     def aggregate(a, b):
         both = jnp.concatenate([row_of(a), row_of(b)], axis=0)
@@ -127,12 +149,6 @@
         part[a] = made[:size]
         part[b] = made[size:]
 
-    def aggregate_first(i):
-        a = at.peer_col(8 - i)
-        aggregate(a, at.peer_col(-7 * i))
-
-    loop(0, 2, aggregate_first)
-
     half_rows = size // 2
 
     def piece(k, half):
@@ -145,11 +161,21 @@
         src = piece(sign * (7 - 2 * t), half)
         return remote(src, side.at[lane, t], rs_send.at[lane, t], rs_recv.at[lane, t], at.at(col=at.peer_col(sign)))
 
-    for lane, sign, half, long in lanes:
-        if long:
-            rc(lane, sign, 0, piece(8 * sign, half)).start()
-    for lane, sign, half, long in lanes:
-        rs(lane, sign, half, 0).start()
+    def first(i):
+        aggregate(at.peer_col(8 - i), at.peer_col(-7 * i))
+
+        @pl.when(i == 0)
+        def _():
+            for lane, sign, half, long in lanes:
+                if long:
+                    rc(lane, sign, 0, piece(8 * sign, half)).start()
+
+        @pl.when(i == 1)
+        def _():
+            for lane, sign, half, long in lanes:
+                rs(lane, sign, half, 0).start()
+
+    loop(0, 2, first)
 
     def rs_step(t):
         loop(0, 2, lambda i: aggregate(at.peer_col(8 - 2 * t - i), at.peer_col(2 * t + i - 8)))
@@ -183,6 +209,8 @@
         halves[half] += side[lane, 3].astype(F32) + chain[lane, 3].astype(F32)
     aggregated = jnp.concatenate(halves, axis=0).astype(BF16)
 
+    load_weight.wait()
+    load_cot.wait()
     preact = jnp.dot(aggregated, weight[...], preferred_element_type=F32)
     sigmoid = jax.nn.sigmoid(preact)
     slopes = sigmoid * (1.0 + preact * (1.0 - sigmoid))
@@ -217,7 +245,7 @@
 
     def columns(rows, q):
         return jnp.concatenate(
-            [jnp.concatenate([adj[idx[r * blocks + 2 * q + i]] for i in range(2)], axis=1) for r in rows], axis=0
+            [jnp.concatenate([block(r, 2 * q + i) for i in range(2)], axis=1) for r in rows], axis=0
         )
 
     def spread(rows):
@@ -239,16 +267,44 @@
     g_sum[...] = g_local[:, at.core] + g_swap[...]
     loop(1, chips, lambda k: g_p(k).start())
 
-    def ag_step(t):
+    group, place = lax.div(me, 4), lax.rem(me, 4)
+
+    def z_peer(k):
+        return at.at(col=group * 4 + lax.rem(place + k, 4))
+
+    def far_peer(k):
+        return at.at(col=lax.rem(group + k, 4) * 4 + place)
+
+    def g_z(k):
+        return remote(z_near.at[place], z_near.at[place], gz_send.at[k], gz_recv, z_peer(k))
+
+    def g_f(k):
+        return remote(z_far.at[group], z_far.at[group], gf_send.at[k], gf_recv, far_peer(k))
+
+    def grad_weight_stage(t):
+        if t == 2:
+            if chips > 1:
+                remote(g_arrived, g_arrived, gp_send.at[0], gp_recv, at.sibling()).wait_recv()
+            total = g_sum[my_chip]
+            for k in range(chips - 1):
+                total += g_arrived[k]
+            z_near[place] = total
+            loop(1, 4, lambda k: g_z(k).start())
+        if t == 3:
+            three = z_near.at[pl.ds(0, 3)]
+            remote(three, three, gz_send.at[0], gz_recv, at.sibling()).wait_recv()
+            z_far[group] = (z_near[0] + z_near[1]) + (z_near[2] + z_near[3])
+            loop(1, 4, lambda k: g_f(k).start())
+
+    for t in range(1, 4):
         for lane, sign, half, long in lanes:
             ac_wait(lane, sign, half, t - 1)
-            if long:
+            if long or t < 3:
                 ac(lane, sign, half, t).start()
-            else:
-                pl.when(t < 3)(lambda: ac(lane, sign, half, t).start())
             as_(lane, sign, half, t).start()
         for lane, sign, half, long in lanes:
             as_wait(lane, sign, half, t - 1)
+        grad_weight_stage(t)
 
         def pair(i):
             k = 2 * t - 1 + i
@@ -257,20 +313,6 @@
                 acc[q] += made(q)
 
         loop(0, 2, pair)
-
-    loop(1, 4, ag_step)
-
-    if chips > 1:
-        remote(g_arrived, g_arrived, gp_send.at[0], gp_recv, at.sibling()).wait_recv()
-    total = g_sum[my_chip]
-    for k in range(chips - 1):
-        total += g_arrived[k]
-    z_buf[me] = total
-
-    def g_z(k):
-        return remote(z_buf.at[me], z_buf.at[me], gz_send.at[k], gz_recv, at.at(col=at.peer_col(k)))
-
-    loop(1, n_col, lambda k: g_z(k).start())
 
     for lane, sign, half, long in lanes:
         as_wait(lane, sign, half, 3)
@@ -300,6 +342,16 @@
             staged.at[h, at.chip(k)], arrived.at[h, k - 1], p_send.at[h, k], p_recv.at[h, k], same_core(k)
         )
 
+    three = z_far.at[pl.ds(0, 3)]
+    remote(three, three, gf_send.at[0], gf_recv, at.sibling()).wait_recv()
+    gw[my_chip, at.core] = ((z_far[0] + z_far[1]) + (z_far[2] + z_far[3])) * scale
+
+    def g_o(k):
+        ref = gw.at[my_chip, at.core]
+        return remote(ref, ref, go_send.at[k], go_recv, same_core(k))
+
+    loop(1, chips, lambda k: g_o(k).start())
+
     sums = []
     for h in range(2):
         swap(h).wait_recv()
@@ -311,18 +363,6 @@
         loop(1, chips, add_and_send)
         sums.append(term(my_chip, h))
 
-    most = z_buf.at[pl.ds(0, n_col - 1)]
-    remote(most, most, gz_send.at[0], gz_recv, at.sibling()).wait_recv()
-    whole = z_buf[0]
-    for k in range(1, n_col):
-        whole += z_buf[k]
-    gw[my_chip, at.core] = whole * scale
-
-    def g_o(k):
-        ref = gw.at[my_chip, at.core]
-        return remote(ref, ref, go_send.at[k], go_recv, same_core(k))
-
-    loop(1, chips, lambda k: g_o(k).start())
     if chips > 1:
         rest = gw.at[pl.ds(0, chips - 1), at.core]
         remote(rest, rest, go_send.at[0], go_recv, at.sibling()).wait_recv()
@@ -347,7 +387,8 @@
             plane(k, h).wait_send()
 
     loop(1, chips, drain)
-    loop(1, n_col, lambda k: g_z(k).wait_send())
+    loop(1, 4, lambda k: g_z(k).wait_send())
+    loop(1, 4, lambda k: g_f(k).wait_send())
     for h in range(2):
         swap(h).wait_send()
 
@@ -362,13 +403,14 @@
         loop(0, 4 if long else 3, lambda t: ac(lane, sign, half, t).wait_send())
 
 
-def whole(idx, mine, weight, cot, adj, n_row, n_col, scale):
+def whole(rows, cols, count, mine, weight, cot, adj, n_row, n_col, scale):
     some, nodes = mine.shape
     slots, size, _ = adj.shape
     width = weight.shape[0]
     chips = n_row // 2
     assert n_col == 16 and nodes % (2 * size) == 0
-    vmem = pl.BlockSpec(memory_space=pltpu.VMEM)
+    smem, vmem, hbm = (pl.BlockSpec(memory_space=m) for m in (pltpu.SMEM, pltpu.VMEM, pl.ANY))
+    table = (n_col * (nodes // size) // 128, 128)
     V = pltpu.VMEM
     few = max(chips - 1, 1)
     return pl.pallas_call(
@@ -378,9 +420,13 @@
             jax.ShapeDtypeStruct((chips, 2, some, width), F32),
             jax.ShapeDtypeStruct((some, nodes), BF16),
         ),
-        in_specs=[pl.BlockSpec(memory_space=pltpu.SMEM), vmem, vmem, vmem, pl.BlockSpec(memory_space=pl.ANY)],
+        in_specs=[smem, smem, smem, vmem, hbm, hbm, hbm],
         out_specs=(vmem,) * 3,
         scratch_shapes=[
+            V(table, jnp.int32),
+            pltpu.SMEM(table, jnp.int32),
+            V((width, width), BF16),
+            V((size, width), BF16),
             V((slots + 1, size, size), BF16),
             V((n_row, some, nodes), BF16),
             V((width, nodes), BF16),
@@ -397,13 +443,14 @@
             V((chips, some, width), F32),
             V((chips, some, width), F32),
             V((few, some, width), F32),
-            V((n_col, some, width), F32),
-            DMA(()),
+            V((4, some, width), F32),
+            V((4, some, width), F32),
+            *[DMA(())] * 4,
             *[DMA((chips,))] * 4,
             *[DMA((4, 4))] * 8,
             DMA(()), DMA(()),
             DMA((chips,)), DMA(()),
-            DMA((n_col,)), DMA(()),
+            DMA((4,)), DMA(()), DMA((4,)), DMA(()),
             DMA((chips,)), DMA(()),
             DMA(()), DMA(()),
             DMA((2,)), DMA((2,)),
@@ -413,15 +460,29 @@
             collective_id=0, has_side_effects=True, vmem_limit_bytes=VMEM_LIMIT
         ),
         name="whole",
-    )(idx, mine, weight, cot, adj)
-
-
-def block_table(rows, cols, count, n_rows, n_cols):
-    slots = rows.shape[0]
-    slot = jnp.arange(slots, dtype=jnp.int32)
-    place = jnp.where(slot < count, rows * n_cols + cols, -1)
-    here = place[:, None] == jnp.arange(n_rows * n_cols, dtype=jnp.int32)[None, :]
-    return jnp.min(jnp.where(here, slot[:, None], slots), axis=0)
+    )(rows, cols, count, mine, weight, cot, adj)
+
+
+def hand_on_kernel(*refs):
+    n = len(refs) // 3
+    copies = [pltpu.make_async_copy(refs[i], refs[n + i], refs[2 * n + i]) for i in range(n)]
+    for copy in copies:
+        copy.start()
+    for copy in copies:
+        copy.wait()
+
+
+def hand_on(*arrays):
+    hbm = pl.BlockSpec(memory_space=pl.ANY)
+    return pl.pallas_call(
+        hand_on_kernel,
+        out_shape=tuple(jax.ShapeDtypeStruct(a.shape, a.dtype) for a in arrays),
+        in_specs=[hbm] * len(arrays),
+        out_specs=(hbm,) * len(arrays),
+        scratch_shapes=[DMA(())] * len(arrays),
+        compiler_params=pltpu.CompilerParams(vmem_limit_bytes=VMEM_LIMIT),
+        name="hand_on",
+    )(*arrays)
 
 
 def solution(mesh):
@@ -430,9 +491,11 @@
     def shards(features, weight, adj_values, block_rows, block_cols, block_counts, cotangent):
         adj = adj_values[0, 0]
         nodes, width = features.shape[0], weight.shape[0]
-        idx = block_table(block_rows[0, 0], block_cols[0, 0], block_counts[0, 0], n_col, nodes // adj.shape[1])
         scale = 1.0 / math.sqrt(nodes * n_col)
-        output, gw, grad = whole(idx, features.T, weight, cotangent, adj, n_row, n_col, scale)
+        made = whole(
+            block_rows[0, 0], block_cols[0, 0], block_counts[0], features.T, weight, cotangent, adj, n_row, n_col, scale
+        )
+        output, gw, grad = hand_on(*made)
         return output, gw.reshape(width, width), grad.T
 
     return jax.shard_map(

time: 108 us -> 111 us (1.028)
  Pallas kernels: 101 us -> 109 us
  local copies, waits for them, and re-layouts: 4.61 us -> 0 us
  other arithmetic: 1.36 us -> 0 us
    pallas_call x0 -> x1, Pallas kernels: none -> 13 us  [hand_on(): pl.pallas_call(hand_on_kernel, out_shape=tuple((jax.ShapeDtypeStruct(a.sh...]
    pallas_call x1, Pallas kernels: 101 us -> 96 us  [whole(): pl.pallas_call(functools.partial(whole_kernel, n_row, n_col, scale), out_...]
    unnamed x3 -> x0, local copies, waits for them, and re-layouts: 4.61 us -> none
where the time goes in v3:
time: 111 us; the launch traced here: 110 us
  Pallas kernels  109 us (98%)
  between operations  1.29 us (1%)
    pallas_call x1, Pallas kernels, whole(): pl.pallas_call(functools.partial(whole_kernel, n_row, n_col, scale), out_...  96 us
    pallas_call x1, Pallas kernels, hand_on(): pl.pallas_call(hand_on_kernel, out_shape=tuple((jax.ShapeDtypeStruct(a.sh...  13 us

profile of v3, /device:TPU:1, one launch (start us, length us, event | category | flops | bytes accessed | tf_op | source)
XLA Modules:
  0.0 110.3 jit_solution(15455008774048601886)
XLA Ops:
  1.3 96.0 %whole.1 = (bf16[128,256]{1,0:T(8,128)(2,1)}, f32[16,2,8,256]{3,2,1,0:T(8,128)}, bf16[8,4096]{1,0:T(8,128)(2,1)}) custom-call(s32[96]{0:T(128)} %bitcast.10, s32[96]{0:T(128)} %bitcast.11, s32[1]{0:T(128)} %bitcast.7.count, bf16[8,4096]{1,0:T(8,128)(2,1)} %bitcast.9, bf16[256,256]{1,0:T(8,128)(2,1)} %weight_hbm.1, bf16[128,256]{1,0:T(8,128)(2,1)} %cot_hbm.1, ...), custom_call_target="tpu_custom_call" | custom-call | tf_op jit(solution)/shard_map/whole/pallas_call | solution.py:416
  97.3 13.0 %hand_on.1 = (bf16[128,256]{1,0:T(8,128)(2,1)}, f32[16,2,8,256]{3,2,1,0:T(8,128)}, bf16[8,4096]{1,0:T(8,128)(2,1)}) custom-call(bf16[128,256]{1,0:T(8,128)(2,1)} %get-tuple-element.9.refs_0_, f32[16,2,8,256]{3,2,1,0:T(8,128)} %get-tuple-element.10.refs_1_, bf16[8,4096]{1,0:T(8,128)(2,1)} %get-tuple-element.11.refs_2_), custom_call_target="tpu_custom_call" | custom-call | tf_op jit(solution)/shard_map/hand_on/pallas_call | solution.py:477

commit v4 on v3

--- a/solution.py
+++ b/solution.py
@@ -100,7 +100,7 @@
 
     lanes_wide = table.shape[1]
     position = lax.broadcasted_iota(jnp.int32, table.shape, 0) * lanes_wide + lax.broadcasted_iota(jnp.int32, table.shape, 1)
-    live = count[0]
+    live = count[0, 0]
 
     def note_slot(s, held):
         place = jnp.where(s < live, rows[s] * blocks + cols[s], -1)
@@ -114,12 +114,15 @@
     def same_core(k):
         return at.at(row=at.chip(k) * 2 + at.core)
 
+    def sent(ref, sem):
+        remote(ref, ref, sem, sem, at.sibling()).wait_send()
+
     def far(k):
-        return remote(mine, gathered.at[at.row], f_send.at[k], f_recv.at[k], same_core(k))
+        return remote(mine, gathered.at[at.row], f_send, f_recv.at[k], same_core(k))
 
     def near(k):
         held = gathered.at[at.chip(k, -1) * 2 + at.core]
-        return remote(held, held, n_send.at[k], n_recv.at[k], at.sibling())
+        return remote(held, held, n_send, n_recv.at[k], at.sibling())
 
     loop(1, chips, lambda k: far(k).start())
     gathered[at.row] = mine[...]
@@ -176,6 +179,10 @@
                 rs(lane, sign, half, 0).start()
 
     loop(0, 2, first)
+
+    sent(gathered.at[pl.ds(0, chips)], n_send)
+    if chips > 1:
+        sent(gathered.at[pl.ds(0, chips - 1)], f_send)
 
     def rs_step(t):
         loop(0, 2, lambda i: aggregate(at.peer_col(8 - 2 * t - i), at.peer_col(2 * t + i - 8)))
@@ -261,9 +268,12 @@
         acc[q] = own(q)
 
     def g_p(k):
-        return remote(g_sum.at[at.chip(k)], g_arrived.at[k - 1], gp_send.at[k], gp_recv, same_core(k))
-
-    g_x.wait_recv()
+        return remote(g_sum.at[at.chip(k)], g_arrived.at[k - 1], gp_send, gp_recv, same_core(k))
+
+    for lane, sign, half, long in lanes:
+        loop(0, 4, lambda t: rs(lane, sign, half, t).wait_send())
+        loop(0 if long else 1, 4, lambda t: rc(lane, sign, t, chain.at[lane, t]).wait_send())
+    g_x.wait()
     g_sum[...] = g_local[:, at.core] + g_swap[...]
     loop(1, chips, lambda k: g_p(k).start())
 
@@ -284,7 +294,7 @@
     def grad_weight_stage(t):
         if t == 2:
             if chips > 1:
-                remote(g_arrived, g_arrived, gp_send.at[0], gp_recv, at.sibling()).wait_recv()
+                remote(g_arrived, g_arrived, gp_send, gp_recv, at.sibling()).wait_recv()
             total = g_sum[my_chip]
             for k in range(chips - 1):
                 total += g_arrived[k]
@@ -339,7 +349,7 @@
 
     def plane(k, h):
         return remote(
-            staged.at[h, at.chip(k)], arrived.at[h, k - 1], p_send.at[h, k], p_recv.at[h, k], same_core(k)
+            staged.at[h, at.chip(k)], arrived.at[h, k - 1], p_send, p_recv.at[h, k], same_core(k)
         )
 
     three = z_far.at[pl.ds(0, 3)]
@@ -348,7 +358,7 @@
 
     def g_o(k):
         ref = gw.at[my_chip, at.core]
-        return remote(ref, ref, go_send.at[k], go_recv, same_core(k))
+        return remote(ref, ref, go_send, go_recv, same_core(k))
 
     loop(1, chips, lambda k: g_o(k).start())
 
@@ -363,12 +373,20 @@
         loop(1, chips, add_and_send)
         sums.append(term(my_chip, h))
 
+    loop(1, 4, lambda k: g_z(k).wait_send())
+    loop(1, 4, lambda k: g_f(k).wait_send())
+    for h in range(2):
+        swap(h).wait_send()
+    for lane, sign, half, long in lanes:
+        loop(0, 4, lambda t: as_(lane, sign, half, t).wait_send())
+        loop(0, 4 if long else 3, lambda t: ac(lane, sign, half, t).wait_send())
+    if chips > 1:
+        sent(g_sum.at[pl.ds(0, chips - 1)], gp_send)
     if chips > 1:
         rest = gw.at[pl.ds(0, chips - 1), at.core]
-        remote(rest, rest, go_send.at[0], go_recv, at.sibling()).wait_recv()
+        remote(rest, rest, go_send, go_recv, at.sibling()).wait_recv()
     g_y = remote(gw.at[:, at.core], gw.at[:, at.core], gy_send, gy_recv, at.sibling())
     g_y.start()
-
     for h in range(2):
         for k in range(1, chips):
             plane(jnp.int32(k), h).wait_recv()
@@ -376,31 +394,10 @@
         grad[:, h * nodes : (h + 1) * nodes] = sums[h].astype(BF16)
     g_y.wait()
 
-    g_x.wait_send()
-    loop(0, chips, lambda k: near(k).wait_send())
-
-    def drain(k):
-        far(k).wait_send()
-        g_p(k).wait_send()
-        g_o(k).wait_send()
-        for h in range(2):
-            plane(k, h).wait_send()
-
-    loop(1, chips, drain)
-    loop(1, 4, lambda k: g_z(k).wait_send())
-    loop(1, 4, lambda k: g_f(k).wait_send())
-    for h in range(2):
-        swap(h).wait_send()
-
-    for lane, sign, half, long in lanes:
-
-        def drain_lane(t):
-            rs(lane, sign, half, t).wait_send()
-            as_(lane, sign, half, t).wait_send()
-
-        loop(0, 4, drain_lane)
-        loop(0 if long else 1, 4, lambda t: rc(lane, sign, t, chain.at[lane, t]).wait_send())
-        loop(0, 4 if long else 3, lambda t: ac(lane, sign, half, t).wait_send())
+    if chips > 1:
+        most = staged.at[:, pl.ds(0, chips - 1)]
+        sent(most, p_send)
+        sent(gw.at[pl.ds(0, chips - 1), at.core], go_send)
 
 
 def whole(rows, cols, count, mine, weight, cot, adj, n_row, n_col, scale):
@@ -446,15 +443,15 @@
             V((4, some, width), F32),
             V((4, some, width), F32),
             *[DMA(())] * 4,
-            *[DMA((chips,))] * 4,
+            DMA(()), DMA((chips,)), DMA(()), DMA((chips,)),
             *[DMA((4, 4))] * 8,
             DMA(()), DMA(()),
-            DMA((chips,)), DMA(()),
+            DMA(()), DMA(()),
             DMA((4,)), DMA(()), DMA((4,)), DMA(()),
-            DMA((chips,)), DMA(()),
+            DMA(()), DMA(()),
             DMA(()), DMA(()),
             DMA((2,)), DMA((2,)),
-            DMA((2, chips)), DMA((2, chips)),
+            DMA(()), DMA((2, chips)),
         ],
         compiler_params=pltpu.CompilerParams(
             collective_id=0, has_side_effects=True, vmem_limit_bytes=VMEM_LIMIT
@@ -464,22 +461,18 @@
 
 
 def hand_on_kernel(*refs):
-    n = len(refs) // 3
-    copies = [pltpu.make_async_copy(refs[i], refs[n + i], refs[2 * n + i]) for i in range(n)]
-    for copy in copies:
-        copy.start()
-    for copy in copies:
-        copy.wait()
+    n = len(refs) // 2
+    for source, target in zip(refs[:n], refs[n:]):
+        target[...] = source[...]
 
 
 def hand_on(*arrays):
-    hbm = pl.BlockSpec(memory_space=pl.ANY)
+    vmem = pl.BlockSpec(memory_space=pltpu.VMEM)
     return pl.pallas_call(
         hand_on_kernel,
         out_shape=tuple(jax.ShapeDtypeStruct(a.shape, a.dtype) for a in arrays),
-        in_specs=[hbm] * len(arrays),
-        out_specs=(hbm,) * len(arrays),
-        scratch_shapes=[DMA(())] * len(arrays),
+        in_specs=[vmem] * len(arrays),
+        out_specs=(vmem,) * len(arrays),
         compiler_params=pltpu.CompilerParams(vmem_limit_bytes=VMEM_LIMIT),
         name="hand_on",
     )(*arrays)
@@ -493,7 +486,7 @@
         nodes, width = features.shape[0], weight.shape[0]
         scale = 1.0 / math.sqrt(nodes * n_col)
         made = whole(
-            block_rows[0, 0], block_cols[0, 0], block_counts[0], features.T, weight, cotangent, adj, n_row, n_col, scale
+            block_rows[0, 0], block_cols[0, 0], block_counts, features.T, weight, cotangent, adj, n_row, n_col, scale
         )
         output, gw, grad = hand_on(*made)
         return output, gw.reshape(width, width), grad.T

time: 111 us -> 98.3 us (0.89)
  Pallas kernels: 109 us -> 96.2 us
    pallas_call x1, Pallas kernels: 13 us -> 1.71 us  [hand_on(): pl.pallas_call(hand_on_kernel, out_shape=tuple((jax.ShapeDtypeStruct(a.sh...]
    pallas_call x1, Pallas kernels: 96 us -> 94.5 us  [whole(): pl.pallas_call(functools.partial(whole_kernel, n_row, n_col, scale), out_...]
where the time goes in v4:
time: 98.3 us; the launch traced here: 97.5 us
  Pallas kernels  96.2 us (98%)
  between operations  1.29 us (1%)
    pallas_call x1, Pallas kernels, whole(): pl.pallas_call(functools.partial(whole_kernel, n_row, n_col, scale), out_...  94.5 us

profile of v4, /device:TPU:1, one launch (start us, length us, event | category | flops | bytes accessed | tf_op | source)
XLA Modules:
  0.0 97.5 jit_solution(10691395253083296078)
XLA Ops:
  1.3 94.5 %whole.1 = (bf16[128,256]{1,0:T(8,128)(2,1)}, f32[16,2,8,256]{3,2,1,0:T(8,128)}, bf16[8,4096]{1,0:T(8,128)(2,1)}) custom-call(s32[96]{0:T(128)} %bitcast.8, s32[96]{0:T(128)} %bitcast.9, s32[1,1]{1,0:T(1,128)S(6)} %copy.10.count, bf16[8,4096]{1,0:T(8,128)(2,1)} %bitcast.7, bf16[256,256]{1,0:T(8,128)(2,1)} %weight_hbm.1, bf16[128,256]{1,0:T(8,128)(2,1)} %cot_hbm.1, ...), custom_call_target="tpu_custom_call" | custom-call | tf_op jit(solution)/shard_map/whole/pallas_call | solution.py:413
  95.8 1.7 %hand_on.1 = (bf16[128,256]{1,0:T(8,128)(2,1)}, f32[16,2,8,256]{3,2,1,0:T(8,128)}, bf16[8,4096]{1,0:T(8,128)(2,1)}) custom-call(bf16[128,256]{1,0:T(8,128)(2,1)} %get-tuple-element.9.refs_0_, f32[16,2,8,256]{3,2,1,0:T(8,128)} %get-tuple-element.10.refs_1_, bf16[8,4096]{1,0:T(8,128)(2,1)} %get-tuple-element.11.refs_2_), custom_call_target="tpu_custom_call" | custom-call | tf_op jit(solution)/shard_map/hand_on/pallas_call | solution.py:471

commit v5 on v4

--- a/solution.py
+++ b/solution.py
@@ -117,25 +117,55 @@
     def sent(ref, sem):
         remote(ref, ref, sem, sem, at.sibling()).wait_send()
 
-    def far(k):
-        return remote(mine, gathered.at[at.row], f_send, f_recv.at[k], same_core(k))
-
-    def near(k):
-        held = gathered.at[at.chip(k, -1) * 2 + at.core]
-        return remote(held, held, n_send, n_recv.at[k], at.sibling())
-
-    loop(1, chips, lambda k: far(k).start())
+    edge = at.side
+    nodes = mine.shape[1] // 2
+    distant = sorted(range(1, edge), key=lambda d: -min(d, edge - d))
+    nearby = distant[::-1]
+
+    def chip(h, a, b):
+        dx, dy = (a, b) if h == 0 else (b, a)
+        return lax.rem(at.x + dx + edge, edge) * edge + lax.rem(at.y + dy + edge, edge)
+
+    def there(h, a, b):
+        return at.at(row=chip(h, a, b) * 2 + at.core)
+
+    def feature(h, a, b):
+        return gathered.at[chip(h, a, b) * 2 + at.core, :, pl.ds(h * nodes, nodes)]
+
+    def first(h, d):
+        return remote(mine.at[:, pl.ds(h * nodes, nodes)], feature(h, 0, 0), f_send, f_recv.at[h, d, 0], there(h, d, 0))
+
+    def second(h, e, d):
+        source = feature(h, -e, 0) if e else mine.at[:, pl.ds(h * nodes, nodes)]
+        return remote(source, feature(h, -e, 0), f_send, f_recv.at[h, e, d], there(h, 0, d))
+
+    def near(h, e, d):
+        return remote(feature(h, -e, -d), feature(h, -e, -d), n_send, n_recv, at.sibling())
+
+    for d in distant:
+        for h in range(2):
+            first(h, d).start()
     gathered[at.row] = mine[...]
-    near(jnp.int32(0)).start()
-
-    def pass_on(k):
-        far(k).wait_recv()
-        near(k).start()
-
-    loop(1, chips, pass_on)
+    for d in distant:
+        for h in range(2):
+            second(h, 0, d).start()
+    for h in range(2):
+        near(h, 0, 0).start()
+    for e in nearby:
+        for h in range(2):
+            first(h, e).wait_recv()
+            for d in distant:
+                second(h, e, d).start()
+            near(h, e, 0).start()
+    for e in (0, *nearby):
+        for d in nearby:
+            for h in range(2):
+                second(h, e, d).wait_recv()
+                near(h, e, d).start()
     load_adj.wait()
     load_table.wait()
-    loop(0, chips, lambda k: near(k).wait_recv())
+    every = gathered.at[pl.ds(0, chips)]
+    remote(every, every, n_send, n_recv, at.sibling()).wait_recv()
     panels[...] = gathered[...].reshape(panels.shape)
 
     per_line = lanes_wide // blocks
@@ -164,7 +194,7 @@
         src = piece(sign * (7 - 2 * t), half)
         return remote(src, side.at[lane, t], rs_send.at[lane, t], rs_recv.at[lane, t], at.at(col=at.peer_col(sign)))
 
-    def first(i):
+    def begin(i):
         aggregate(at.peer_col(8 - i), at.peer_col(-7 * i))
 
         @pl.when(i == 0)
@@ -178,7 +208,7 @@
             for lane, sign, half, long in lanes:
                 rs(lane, sign, half, 0).start()
 
-    loop(0, 2, first)
+    loop(0, 2, begin)
 
     sent(gathered.at[pl.ds(0, chips)], n_send)
     if chips > 1:
@@ -330,8 +360,6 @@
         if long:
             ac_wait(lane, sign, half, 3)
 
-    nodes = terms.shape[3] // 2
-
     def swap(h):
         return remote(
             terms.at[:, 1 - at.core, :, pl.ds(h * nodes, nodes)], swapped.at[h], x_send.at[h], x_recv.at[h], at.sibling()
@@ -347,10 +375,13 @@
     def term(c, h):
         return terms[c, at.core, :, h * nodes : (h + 1) * nodes].astype(F32) + swapped[h, c].astype(F32)
 
-    def plane(k, h):
-        return remote(
-            staged.at[h, at.chip(k)], arrived.at[h, k - 1], p_send, p_recv.at[h, k], same_core(k)
-        )
+    def along_first(h, d, b):
+        slot = (d - 1) * edge + b
+        return remote(staged.at[h, chip(h, d, b)], arrived.at[h, slot], p_send, p_recv.at[h, slot], there(h, d, 0))
+
+    def along_second(h, b):
+        slot = (edge - 1) * edge + b - 1
+        return remote(staged.at[h, chip(h, 0, b)], arrived.at[h, slot], p_send, p_recv.at[h, slot], there(h, 0, b))
 
     three = z_far.at[pl.ds(0, 3)]
     remote(three, three, gf_send.at[0], gf_recv, at.sibling()).wait_recv()
@@ -362,16 +393,24 @@
 
     loop(1, chips, lambda k: g_o(k).start())
 
-    sums = []
     for h in range(2):
         swap(h).wait_recv()
-
-        def add_and_send(k):
-            staged[h, at.chip(k)] = term(at.chip(k), h).astype(BF16)
-            plane(k, h).start()
-
-        loop(1, chips, add_and_send)
-        sums.append(term(my_chip, h))
+        for b in (*distant, 0):
+            for d in distant:
+                staged[h, chip(h, d, b)] = term(chip(h, d, b), h).astype(BF16)
+                along_first(h, d, b).start()
+
+    def gathered_sum(h, b):
+        total = term(chip(h, 0, b), h)
+        for d in nearby:
+            along_first(h, d, b).wait_recv()
+            total += arrived[h, (d - 1) * edge + b].astype(F32)
+        return total
+
+    for b in distant:
+        for h in range(2):
+            staged[h, chip(h, 0, b)] = gathered_sum(h, b).astype(BF16)
+            along_second(h, b).start()
 
     loop(1, 4, lambda k: g_z(k).wait_send())
     loop(1, 4, lambda k: g_f(k).wait_send())
@@ -388,10 +427,11 @@
     g_y = remote(gw.at[:, at.core], gw.at[:, at.core], gy_send, gy_recv, at.sibling())
     g_y.start()
     for h in range(2):
-        for k in range(1, chips):
-            plane(jnp.int32(k), h).wait_recv()
-            sums[h] += arrived[h, k - 1].astype(F32)
-        grad[:, h * nodes : (h + 1) * nodes] = sums[h].astype(BF16)
+        total = gathered_sum(h, 0)
+        for b in nearby:
+            along_second(h, b).wait_recv()
+            total += arrived[h, (edge - 1) * edge + b - 1].astype(F32)
+        grad[:, h * nodes : (h + 1) * nodes] = total.astype(BF16)
     g_y.wait()
 
     if chips > 1:
@@ -405,6 +445,7 @@
     slots, size, _ = adj.shape
     width = weight.shape[0]
     chips = n_row // 2
+    side = math.isqrt(chips)
     assert n_col == 16 and nodes % (2 * size) == 0
     smem, vmem, hbm = (pl.BlockSpec(memory_space=m) for m in (pltpu.SMEM, pltpu.VMEM, pl.ANY))
     table = (n_col * (nodes // size) // 128, 128)
@@ -443,7 +484,7 @@
             V((4, some, width), F32),
             V((4, some, width), F32),
             *[DMA(())] * 4,
-            DMA(()), DMA((chips,)), DMA(()), DMA((chips,)),
+            DMA(()), DMA((2, side, side)), DMA(()), DMA(()),
             *[DMA((4, 4))] * 8,
             DMA(()), DMA(()),
             DMA(()), DMA(()),

time: 98.3 us -> 89.8 us (0.914)
  Pallas kernels: 96.2 us -> 88.3 us
    pallas_call x1, Pallas kernels: 94.5 us -> 86.6 us  [whole(): pl.pallas_call(functools.partial(whole_kernel, n_row, n_col, scale), out_...]
where the time goes in v5:
time: 89.8 us; the launch traced here: 89.6 us
  Pallas kernels  88.3 us (98%)
  between operations  1.29 us (1%)
    pallas_call x1, Pallas kernels, whole(): pl.pallas_call(functools.partial(whole_kernel, n_row, n_col, scale), out_...  86.6 us

profile of v5, /device:TPU:1, one launch (start us, length us, event | category | flops | bytes accessed | tf_op | source)
XLA Modules:
  0.0 89.6 jit_solution(7395970963319609763)
XLA Ops:
  1.3 86.6 %whole.1 = (bf16[128,256]{1,0:T(8,128)(2,1)}, f32[16,2,8,256]{3,2,1,0:T(8,128)}, bf16[8,4096]{1,0:T(8,128)(2,1)}) custom-call(s32[96]{0:T(128)} %bitcast.8, s32[96]{0:T(128)} %bitcast.9, s32[1,1]{1,0:T(1,128)S(6)} %copy.10.count, bf16[8,4096]{1,0:T(8,128)(2,1)} %bitcast.7, bf16[256,256]{1,0:T(8,128)(2,1)} %weight_hbm.1, bf16[128,256]{1,0:T(8,128)(2,1)} %cot_hbm.1, ...), custom_call_target="tpu_custom_call" | custom-call | tf_op jit(solution)/shard_map/whole/pallas_call | solution.py:454
  87.9 1.7 %hand_on.1 = (bf16[128,256]{1,0:T(8,128)(2,1)}, f32[16,2,8,256]{3,2,1,0:T(8,128)}, bf16[8,4096]{1,0:T(8,128)(2,1)}) custom-call(bf16[128,256]{1,0:T(8,128)(2,1)} %get-tuple-element.9.refs_0_, f32[16,2,8,256]{3,2,1,0:T(8,128)} %get-tuple-element.10.refs_1_, bf16[8,4096]{1,0:T(8,128)(2,1)} %get-tuple-element.11.refs_2_), custom_call_target="tpu_custom_call" | custom-call | tf_op jit(solution)/shard_map/hand_on/pallas_call | solution.py:512

commit v6 on v5

--- a/solution.py
+++ b/solution.py
@@ -9,7 +9,7 @@
 from jax.sharding import PartitionSpec as P
 
 MESH = pl.DeviceIdType.MESH
-VMEM_LIMIT = 56 * 2**20
+VMEM_LIMIT = 52 * 2**20
 NT = (((1,), (1,)), ((), ()))
 TN = (((0,), (0,)), ((), ()))
 DMA = pltpu.SemaphoreType.DMA
@@ -63,17 +63,22 @@
     lax.fori_loop(start, stop, step, 0)
 
 
+PIECES = 2
+
+
 def lanes_of():
-    return [(2 * way + half, 1 - 2 * way, half, way == half) for half in range(2) for way in range(2)]
+    return [
+        (PIECES * way + piece, 1 - 2 * way, piece, way == piece % 2) for piece in range(PIECES) for way in range(2)
+    ]
 
 
 def whole_kernel(
     n_row, n_col, scale,
-    rows, cols, count, mine, weight_hbm, cot_hbm, adj_hbm,
+    rows_hbm, cols_hbm, count_hbm, mine, weight_hbm, cot_hbm, adj_hbm,
     output, gw, grad,
-    table, idx, weight, cot, adj, gathered, panels, part, chain, side, back, acc, terms, swapped, staged, arrived,
+    rows, cols, count, table, idx, weight, cot, adj, gathered, panels, part, chain, side, back, acc, terms, swapped, staged, arrived,
     g_local, g_swap, g_sum, g_arrived, z_near, z_far,
-    table_sem, weight_sem, cot_sem, adj_sem, f_send, f_recv, n_send, n_recv, rc_send, rc_recv, rs_send, rs_recv, ac_send, ac_recv, as_send, as_recv,
+    tile_sem, table_sem, weight_sem, cot_sem, adj_sem, f_send, f_recv, n_send, n_recv, rc_send, rc_recv, rs_send, rs_recv, ac_send, ac_recv, as_send, as_recv,
     gx_send, gx_recv, gp_send, gp_recv, gz_send, gz_recv, gf_send, gf_recv, go_send, go_recv, gy_send, gy_recv,
     x_send, x_recv, p_send, p_recv,
 ):
@@ -88,6 +93,10 @@
     load_adj = pltpu.make_async_copy(adj_hbm, adj.at[pl.ds(0, slots)], adj_sem)
     load_weight = pltpu.make_async_copy(weight_hbm, weight, weight_sem)
     load_cot = pltpu.make_async_copy(cot_hbm, cot, cot_sem)
+    tile = ((rows_hbm, rows), (cols_hbm, cols), (count_hbm, count))
+    load_tile = [pltpu.make_async_copy(a, b, tile_sem.at[i]) for i, (a, b) in enumerate(tile)]
+    for load in load_tile:
+        load.start()
     load_adj.start()
     load_weight.start()
     load_cot.start()
@@ -100,10 +109,12 @@
 
     lanes_wide = table.shape[1]
     position = lax.broadcasted_iota(jnp.int32, table.shape, 0) * lanes_wide + lax.broadcasted_iota(jnp.int32, table.shape, 1)
+    for load in load_tile:
+        load.wait()
     live = count[0, 0]
 
     def note_slot(s, held):
-        place = jnp.where(s < live, rows[s] * blocks + cols[s], -1)
+        place = jnp.where(s < live, rows[0, s] * blocks + cols[0, s], -1)
         return jnp.where(position == place, s, held)
 
     table[...] = lax.fori_loop(0, slots, note_slot, jnp.full(table.shape, slots, jnp.int32))
@@ -182,7 +193,7 @@
         part[a] = made[:size]
         part[b] = made[size:]
 
-    half_rows = size // 2
+    half_rows = size // PIECES
 
     def piece(k, half):
         return part.at[at.peer_col(k), pl.ds(half * half_rows, half_rows)]
@@ -239,7 +250,7 @@
             rs(lane, sign, half, t).start()
 
     loop(1, 4, rs_step)
-    halves = [part[me, h * half_rows : (h + 1) * half_rows].astype(F32) for h in range(2)]
+    halves = [part[me, h * half_rows : (h + 1) * half_rows].astype(F32) for h in range(PIECES)]
     for lane, sign, half, long in lanes:
         rs(lane, sign, half, 3).wait_recv()
         rc(lane, sign, 3, chain.at[lane, 3]).wait_recv()
@@ -254,7 +265,7 @@
     deltas = (cot[...].astype(F32) * slopes).astype(BF16)
     back[me] = lax.dot_general(weight[...], deltas, NT, preferred_element_type=F32).astype(BF16)
 
-    half_back = width // 2
+    half_back = width // PIECES
 
     def held(k, half):
         return back.at[at.peer_col(k), pl.ds(half * half_back, half_back)]
@@ -360,17 +371,19 @@
         if long:
             ac_wait(lane, sign, half, 3)
 
-    def swap(h):
-        return remote(
-            terms.at[:, 1 - at.core, :, pl.ds(h * nodes, nodes)], swapped.at[h], x_send.at[h], x_recv.at[h], at.sibling()
-        )
+    quarter = nodes // 2
+
+    def swap(p):
+        there_to = swapped.at[p // 2, :, :, pl.ds(p % 2 * quarter, quarter)]
+        source = terms.at[:, 1 - at.core, :, pl.ds(p * quarter, quarter)]
+        return remote(source, there_to, x_send.at[p], x_recv.at[p], at.sibling())
 
     last = spread([at.peer_col(7), at.peer_col(-7), at.peer_col(8)])
     for q in range(blocks // 2):
         made = (acc[q] + last(q)).astype(BF16)
         terms[:, :, :, q * 2 * size : (q + 1) * 2 * size] = made.reshape(*terms.shape[:3], 2 * size)
-        if (q + 1) % (blocks // 4) == 0:
-            swap((q + 1) // (blocks // 4) - 1).start()
+        if (q + 1) % (blocks // 8) == 0:
+            swap((q + 1) // (blocks // 8) - 1).start()
 
     def term(c, h):
         return terms[c, at.core, :, h * nodes : (h + 1) * nodes].astype(F32) + swapped[h, c].astype(F32)
@@ -383,22 +396,25 @@
         slot = (edge - 1) * edge + b - 1
         return remote(staged.at[h, chip(h, 0, b)], arrived.at[h, slot], p_send, p_recv.at[h, slot], there(h, 0, b))
 
-    three = z_far.at[pl.ds(0, 3)]
-    remote(three, three, gf_send.at[0], gf_recv, at.sibling()).wait_recv()
-    gw[my_chip, at.core] = ((z_far[0] + z_far[1]) + (z_far[2] + z_far[3])) * scale
-
     def g_o(k):
         ref = gw.at[my_chip, at.core]
         return remote(ref, ref, go_send, go_recv, same_core(k))
 
-    loop(1, chips, lambda k: g_o(k).start())
+    def grad_weight_out():
+        three = z_far.at[pl.ds(0, 3)]
+        remote(three, three, gf_send.at[0], gf_recv, at.sibling()).wait_recv()
+        gw[my_chip, at.core] = ((z_far[0] + z_far[1]) + (z_far[2] + z_far[3])) * scale
+        loop(1, chips, lambda k: g_o(k).start())
 
     for h in range(2):
-        swap(h).wait_recv()
+        swap(2 * h).wait_recv()
+        swap(2 * h + 1).wait_recv()
         for b in (*distant, 0):
             for d in distant:
                 staged[h, chip(h, d, b)] = term(chip(h, d, b), h).astype(BF16)
                 along_first(h, d, b).start()
+        if h == 0:
+            grad_weight_out()
 
     def gathered_sum(h, b):
         total = term(chip(h, 0, b), h)
@@ -414,8 +430,8 @@
 
     loop(1, 4, lambda k: g_z(k).wait_send())
     loop(1, 4, lambda k: g_f(k).wait_send())
-    for h in range(2):
-        swap(h).wait_send()
+    for p in range(4):
+        swap(p).wait_send()
     for lane, sign, half, long in lanes:
         loop(0, 4, lambda t: as_(lane, sign, half, t).wait_send())
         loop(0, 4 if long else 3, lambda t: ac(lane, sign, half, t).wait_send())
@@ -447,7 +463,7 @@
     chips = n_row // 2
     side = math.isqrt(chips)
     assert n_col == 16 and nodes % (2 * size) == 0
-    smem, vmem, hbm = (pl.BlockSpec(memory_space=m) for m in (pltpu.SMEM, pltpu.VMEM, pl.ANY))
+    vmem, hbm = (pl.BlockSpec(memory_space=m) for m in (pltpu.VMEM, pltpu.HBM))
     table = (n_col * (nodes // size) // 128, 128)
     V = pltpu.VMEM
     few = max(chips - 1, 1)
@@ -458,9 +474,12 @@
             jax.ShapeDtypeStruct((chips, 2, some, width), F32),
             jax.ShapeDtypeStruct((some, nodes), BF16),
         ),
-        in_specs=[smem, smem, smem, vmem, hbm, hbm, hbm],
+        in_specs=[hbm, hbm, hbm, vmem, hbm, hbm, hbm],
         out_specs=(vmem,) * 3,
         scratch_shapes=[
+            pltpu.SMEM((1, slots), jnp.int32),
+            pltpu.SMEM((1, slots), jnp.int32),
+            pltpu.SMEM((1, 1), jnp.int32),
             V(table, jnp.int32),
             pltpu.SMEM(table, jnp.int32),
             V((width, width), BF16),
@@ -469,8 +488,8 @@
             V((n_row, some, nodes), BF16),
             V((width, nodes), BF16),
             V((n_col, size, width), BF16),
-            V((4, 4, size // 2, width), BF16),
-            V((4, 4, size // 2, width), BF16),
+            V((2 * PIECES, 4, size // PIECES, width), BF16),
+            V((2 * PIECES, 4, size // PIECES, width), BF16),
             V((n_col, width, size), BF16),
             V((nodes // (2 * size), width, 2 * size), F32),
             V((chips, 2, some, nodes), BF16),
@@ -483,15 +502,16 @@
             V((few, some, width), F32),
             V((4, some, width), F32),
             V((4, some, width), F32),
+            DMA((3,)),
             *[DMA(())] * 4,
             DMA(()), DMA((2, side, side)), DMA(()), DMA(()),
-            *[DMA((4, 4))] * 8,
+            *[DMA((2 * PIECES, 4))] * 8,
             DMA(()), DMA(()),
             DMA(()), DMA(()),
             DMA((4,)), DMA(()), DMA((4,)), DMA(()),
             DMA(()), DMA(()),
             DMA(()), DMA(()),
-            DMA((2,)), DMA((2,)),
+            DMA((4,)), DMA((4,)),
             DMA(()), DMA((2, chips)),
         ],
         compiler_params=pltpu.CompilerParams(
@@ -514,7 +534,7 @@
         out_shape=tuple(jax.ShapeDtypeStruct(a.shape, a.dtype) for a in arrays),
         in_specs=[vmem] * len(arrays),
         out_specs=(vmem,) * len(arrays),
-        compiler_params=pltpu.CompilerParams(vmem_limit_bytes=VMEM_LIMIT),
+        compiler_params=pltpu.CompilerParams(vmem_limit_bytes=4 * 2**20),
         name="hand_on",
     )(*arrays)
 
@@ -527,7 +547,7 @@
         nodes, width = features.shape[0], weight.shape[0]
         scale = 1.0 / math.sqrt(nodes * n_col)
         made = whole(
-            block_rows[0, 0], block_cols[0, 0], block_counts, features.T, weight, cotangent, adj, n_row, n_col, scale
+            block_rows[0], block_cols[0], block_counts, features.T, weight, cotangent, adj, n_row, n_col, scale
         )
         output, gw, grad = hand_on(*made)
         return output, gw.reshape(width, width), grad.T

time: 89.8 us -> 92.3 us (1.028)
  local copies, waits for them, and re-layouts: 0 us -> 3.88 us
  Pallas kernels: 88.3 us -> 86.9 us
    unnamed x0 -> x10, local copies, waits for them, and re-layouts: none -> 3.88 us
    pallas_call x1, Pallas kernels: 1.71 us -> 0.76 us  [hand_on(): pl.pallas_call(hand_on_kernel, out_shape=tuple((jax.ShapeDtypeStruct(a.sh...]
where the time goes in v6:
time: 92.3 us; the launch traced here: 92.1 us
  Pallas kernels  86.9 us (94%)
  local copies, waits for them, and re-layouts  3.88 us (4%)
  between operations  1.3 us (1%)
    pallas_call x1, Pallas kernels, whole(): pl.pallas_call(functools.partial(whole_kernel, n_row, n_col, scale), out_...  86.1 us
    unnamed x10, local copies, waits for them, and re-layouts  3.88 us

profile of v6, /device:TPU:1, one launch (start us, length us, event | category | flops | bytes accessed | tf_op | source)
XLA Modules:
  0.0 92.1 jit_solution(9053915927040643205)
XLA Ops:
  1.3 0.0 copy-start
  1.3 0.9 copy-done
  2.2 0.0 copy-start.1
  2.2 0.8 copy-done.1
  3.0 0.0 copy-start.2
  3.0 0.8 copy-done.2
  3.9 0.0 copy-start.3
  3.9 0.7 copy-done.3
  4.5 0.0 copy-start.4
  4.5 0.7 copy-done.4
  5.2 86.1 %whole.1 = (bf16[128,256]{1,0:T(8,128)(2,1)S(1)}, f32[16,2,8,256]{3,2,1,0:T(8,128)S(1)}, bf16[8,4096]{1,0:T(8,128)(2,1)S(1)}) custom-call(s32[1,96]{1,0:T(1,128)S(1)} %bitcast.7, s32[1,96]{1,0:T(1,128)S(1)} %bitcast.8, s32[1,1]{1,0:T(1,128)S(6)} %copy.10.count_hbm, bf16[8,4096]{1,0:T(8,128)(2,1)S(1)} %bitcast.6, bf16[256,256]{1,0:T(8,128)(2,1)S(1)} %copy-done, ...), custom_call_target="tpu_custom_call" | custom-call | tf_op jit(solution)/shard_map/whole/pallas_call | solution.py:470
  91.3 0.8 hand_on.1
Async XLA Ops:
  1.3 0.9 copy-start
  2.2 0.8 copy-start.1
  3.0 0.8 copy-start.2
  3.9 0.7 copy-start.3
  4.5 0.7 copy-start.4
